TPU v7x, 32 devices: a whole 2x2x4 slice. The times are simulated.
32 devices in a mesh: row: 8 (over z, y), col: 4 (over x, core).
Axes of the slice: x: 2, y: 2, z: 4, core: 2. Of those that a mesh axis runs over, the one named last changes fastest.
Arguments:
- amplitudes: float32 [1024, 128, 128], P(('row', 'col')), may hold values from -6 to 6
- amp_owner: int32 [1024, 1], P(('row', 'col')), may hold values from 0 to 31; in each aligned block of 32 rows (0 to 31, 32 to 63, ...) at most 2 rows name the same one
- amp_occ: int32 [1024], P(('row', 'col')), may hold values from 0 to 11
- amp_vir: int32 [1024], P(('row', 'col')), may hold values from 0 to 31
- integrals: float32 [16384, 4, 128], P('col'), may hold values from -0.15625 to 0.15625
Outputs:
- residual: float32 [4, 12288, 128], P('col', 'row')
Inputs may be any that keep to these rules, and one draw needn't show every extreme that they name: `amp_owner`: among the tiles listed on one device no owner is named more than 2 times, a bound that some block reaches.
All inputs are finite; a program needn't handle non-finite values.
Results may differ from a plain program's by a relative error of at most 0.0003.
Values sent between devices are 32-bit elements; how exact they have to be, the bound alone decides.
No kernel may reach another device: no remote copies, remote signals or barrier semaphores. Data moves between devices by JAX's collectives and lax.ppermute only.
A program may use at most 192 MiB of HBM per device.

v0:
```python
import jax
import jax.numpy as jnp
from jax import lax
from jax.sharding import PartitionSpec as P

CAP = 2
OCC_DEV = 12
CV_DEV = 32


def body(amplitudes, amp_owner, amp_occ, amp_vir, integrals):
    rows_count = lax.axis_size("row")
    cols_count = lax.axis_size("col")
    devices = rows_count * cols_count
    listed = amplitudes.shape[0]
    tile = amplitudes.shape[1]
    owner = amp_owner[:, 0]
    positions = jnp.arange(listed, dtype=jnp.int32)
    earlier = (owner[None, :] == owner[:, None]) & (positions[None, :] < positions[:, None])
    rank = jnp.sum(earlier.astype(jnp.int32), axis=1)
    slot = owner * CAP + rank
    pair = amp_occ * CV_DEV + amp_vir
    send_tiles = jnp.zeros((devices * CAP, tile, tile), jnp.float32).at[slot].set(amplitudes)
    send_pairs = jnp.zeros((devices * CAP,), jnp.int32).at[slot].set(pair)
    got_tiles, got_pairs = (
        lax.all_to_all(send_tiles, ("row", "col"), split_axis=0, concat_axis=0, tiled=True),
        lax.all_to_all(send_pairs, ("row", "col"), split_axis=0, concat_axis=0, tiled=True),
    )
    grid = jnp.zeros((OCC_DEV * CV_DEV, tile, tile), jnp.float32).at[got_pairs].add(got_tiles)
    grid = grid.reshape(OCC_DEV, CV_DEV, tile, tile)
    out_tiles = integrals.shape[1]
    blocks = integrals.reshape(CV_DEV, tile, out_tiles, tile)
    own_tiles = out_tiles // cols_count
    result = jnp.einsum("pcij,cjak->apik", grid, blocks, precision=lax.Precision.HIGHEST)
    return lax.psum_scatter(
        result.reshape(own_tiles * lax.axis_size("col"), OCC_DEV * tile, tile),
        "col",
        scatter_dimension=0,
        tiled=True,
    )


def solution(mesh):
    in_specs = (
        P(("row", "col"), None, None),
        P(("row", "col"), None),
        P(("row", "col")),
        P(("row", "col")),
        P("col", None, None),
    )
    out_specs = P("col", "row", None)
    return jax.shard_map(body, mesh=mesh, in_specs=in_specs, out_specs=out_specs, check_vma=False)
```

profile of v0, /device:TPU:0, one launch (start us, length us, event | category | flops | bytes accessed | tf_op | source)
XLA Modules:
  0.0 242.5 jit_solution(1448802218985810424)
XLA Ops:
  6.5 0.0 copy-start
  6.5 1.0 convert_reduce_fusion
  7.5 0.7 fusion.7
  8.2 0.7 multiply_add_fusion
  8.9 0.7 scatter_custom_fusion
  9.6 0.7 all_to_all.11
  10.3 7.3 %all-to-all-start = ((s32[32,2,1]{1,2,0:T(1,128)}), s32[32,2,1]{1,2,0:T(1,128)S(1)}, u32[]{:S(2)}, u32[]{:S(2)}) async-start(s32[32,2,1]{1,2,0:T(1,128)} %bitcast.3), calls=%async_computation | async-start | bytes 32768 | tf_op jit(solution)/shard_map/all_to_all | solution.py:27
  17.6 2.4 %broadcast_in_dim.5 = f32[64,128,128]{2,1,0:T(8,128)} broadcast(f32[]{:T(128)} %constant.6.clone.1), dimensions={} | broadcast | bytes 4194308 | tf_op jit(solution)/shard_map/broadcast_in_dim | solution.py:23
  20.0 0.0 copy-done
  20.0 5.4 %scatter_fusion = f32[64,128,128]{2,1,0:T(8,128)} fusion(f32[64,128,128]{2,1,0:T(8,128)} %broadcast_in_dim.5, s32[32]{0:T(128)S(1)} %fusion.7, f32[32,128,128]{2,1,0:T(8,128)S(1)} %copy-done), kind=kCustom, calls=%fused_computation.1 | custom fusion | bytes 6291584 | tf_op jit(solution)/shard_map/scatter | solution.py:23
  25.4 0.0 all-to-all-done
  25.4 6.0 %all-to-all-start.1 = ((f32[64,128,128]{2,1,0:T(8,128)}), f32[64,128,128]{2,1,0:T(8,128)}, u32[]{:S(2)}, u32[]{:S(2)}) async-start(f32[64,128,128]{2,1,0:T(8,128)} %scatter_fusion), calls=%async_computation.1 | async-start | bytes 8388608 | tf_op jit(solution)/shard_map/all_to_all | solution.py:26
  31.4 0.0 reduce-scatter.2.cloned.1.call-start
  31.5 0.5 broadcast.40
  32.0 0.7 reduce.3
  32.7 0.1 all_to_all.13
  32.8 92.5 %all-to-all-done.1 = f32[64,128,128]{2,1,0:T(8,128)} async-done(((f32[64,128,128]{2,1,0:T(8,128)}), f32[64,128,128]{2,1,0:T(8,128)}, u32[]{:S(2)}, u32[]{:S(2)}) %all-to-all-start.1) | async-done | bytes 4194336 | tf_op jit(solution)/shard_map/all_to_all | solution.py:26
  125.3 11.5 %broadcast_in_dim.4 = f32[384,128,128]{2,1,0:T(8,128)} broadcast(f32[]{:T(128)} %constant.6.clone.1), dimensions={} | broadcast | bytes 25165828 | tf_op jit(solution)/shard_map/broadcast_in_dim | solution.py:29
  136.8 13.6 %scatter_fusion.1 = f32[384,128,128]{2,1,0:T(8,128)} fusion(f32[384,128,128]{2,1,0:T(8,128)} %broadcast_in_dim.4, s32[64]{0:T(128)S(1)} %fusion.8, f32[64,128,128]{2,1,0:T(8,128)} %all-to-all-done.1), kind=kCustom, calls=%fused_computation.2 | custom fusion | flops 1048576 | bytes 12583168 | tf_op jit(solution)/shard_map/scatter-add | solution.py:29
  150.4 46.1 %fusion.3 = f32[4,12,128,128]{3,2,0,1:T(8,128)S(1)} fusion(f32[12,32,128,128,1]{3,2,1,4,0:T(8,128)} %bitcast.31, f32[32,128,4,128]{3,2,1,0:T(4,128)} %bitcast.33), kind=kOutput, calls=%fused_computation.6 | convolution fusion | flops 38654705664 | bytes 36700160 | tf_op jit(solution)/shard_map/pcij,cjak->apik/dot_general | solution.py:34
  196.5 1.9 copy.14
  198.4 0.0 reduce-scatter.2.cloned.1.call-update
  198.4 37.2 %reduce-scatter.2.cloned.1.call-done = f32[1,1536,128]{2,1,0:T(8,128)} async-done(((f32[4,1536,128]{2,1,0:T(8,128)}), f32[1,1536,128]{2,1,0:T(8,128)}) %reduce-scatter.2.cloned.1.call-update) | async-done | bytes 786448 | tf_op jit(solution)/shard_map/reduce_scatter | solution.py:35
  (1 shorter events, 0.0 us)
Async XLA Ops:
  6.5 13.5 %copy-start = (f32[32,128,128]{2,1,0:T(8,128)S(1)}, f32[32,128,128]{2,1,0:T(8,128)}, u32[]{:S(2)}) copy-start(f32[32,128,128]{2,1,0:T(8,128)} %param.5) | copy-start | bytes 6291460
  10.3 15.1 %all-to-all-start = ((s32[32,2,1]{1,2,0:T(1,128)}), s32[32,2,1]{1,2,0:T(1,128)S(1)}, u32[]{:S(2)}, u32[]{:S(2)}) async-start(s32[32,2,1]{1,2,0:T(1,128)} %bitcast.3), calls=%async_computation | async-start | bytes 32768 | tf_op jit(solution)/shard_map/all_to_all | solution.py:27
  25.4 99.9 %all-to-all-start.1 = ((f32[64,128,128]{2,1,0:T(8,128)}), f32[64,128,128]{2,1,0:T(8,128)}, u32[]{:S(2)}, u32[]{:S(2)}) async-start(f32[64,128,128]{2,1,0:T(8,128)} %scatter_fusion), calls=%async_computation.1 | async-start | bytes 8388608 | tf_op jit(solution)/shard_map/all_to_all | solution.py:26
  31.4 204.2 %reduce-scatter.2.cloned.1.call-start = ((), (), s32[]{:S(2)}) async-start(), calls=%async_computation.3 | async-start | bytes 3932160 | tf_op jit(solution)/shard_map/reduce_scatter | solution.py:35
Sparse Core Ops, SparseCore 0:
  198.5 37.0 reduce-scatter.1
where the time goes:
time: 243 us; the launch traced here: 242 us
  waiting for transfers between devices  130 us (53%)
  matrix products  46.1 us (19%)
  local copies, waits for them, and re-layouts  23.2 us (10%)
  other arithmetic  16.6 us (7%)
  between operations  13.5 us (6%)
  starting transfers between devices  13.4 us (6%)
    all_to_all x1, waiting for transfers between devices, body(): lax.all_to_all(send_tiles, ('row', 'col'), split_axis=0, concat_axis=0, t...  92.5 us
    dot_general x1, matrix products, body(): jnp.einsum('pcij,cjak->apik', grid, blocks, precision=lax.Precision.HIGHEST)  46.1 us
    reduce_scatter x1, waiting for transfers between devices, body(): lax.psum_scatter(result.reshape(own_tiles * lax.axis_size('col'), OCC_DEV...  37.2 us
    scatter-add x1, other arithmetic, body(): jnp.zeros((OCC_DEV * CV_DEV, tile, tile), jnp.float32).at[got_pairs]  13.6 us
    broadcast_in_dim x1, local copies, waits for them, and re-layouts, body(): jnp.zeros((OCC_DEV * CV_DEV, tile, tile), jnp.float32).at[got_pairs]  11.5 us
    all_to_all x1, starting transfers between devices, body(): lax.all_to_all(send_pairs, ('row', 'col'), split_axis=0, concat_axis=0, t...  7.3 us
    all_to_all x1, starting transfers between devices, body(): lax.all_to_all(send_tiles, ('row', 'col'), split_axis=0, concat_axis=0, t...  6.02 us
    scatter x1, local copies, waits for them, and re-layouts, body(): jnp.zeros((devices * CAP, tile, tile), jnp.float32).at[slot].set(amplitudes)  5.38 us
  transfers between devices with their start and end apart: 3, of which 2 were waited for; matrix products, arithmetic and copies ran while one was open for 4% of the time, Pallas kernels for 0%

commit v1 on v0

v1 whole, which is shorter than its diff:
```python
import functools
import math

import jax
import jax.numpy as jnp
from jax import lax
from jax.experimental import pallas as pl
from jax.experimental.pallas import tpu as pltpu
from jax.sharding import PartitionSpec as P

CAP = 2
OCC_DEV = 12
CV_DEV = 32
CV_BITS = CV_DEV.bit_length() - 1
NZ = 4
PIECES = 4
HEAD = 8
SPANS = (5, 7)
SHIFT = 9
MASK = (1 << SHIFT) - 1
GROUP = 4
SLOTS = 4
AXES = ("row", "col")
ANY = pl.BlockSpec(memory_space=pl.ANY)
f32 = jnp.float32
bf16 = jnp.bfloat16


def room(*arrays):
    return sum(4 * math.prod(a) for a in arrays) + (6 << 20)


def pack_kernel(tiles, devices, per_round, rnd, owner, occ, vir, amp, send, pay, held, count, head, sem_in, sem_a, sem_b, sem_h):
    edge = amp.shape[1]
    piece = tiles // PIECES
    loads = [pltpu.make_async_copy(amp.at[pl.ds(i * piece, piece)], held.at[pl.ds(i * piece, piece)], sem_in.at[i]) for i in range(PIECES)]
    for load in loads:
        load.start()

    def clear(d, c):
        count[d] = 0
        head[0, d] = 0.0
        return c

    lax.fori_loop(0, devices, clear, 0, unroll=8)
    base = rnd[0] * per_round

    def first(t, d):
        return pltpu.make_async_copy(held.at[t], send.at[d], sem_a.at[d])

    def second(t, j):
        return pltpu.make_async_copy(held.at[t], pay.at[pl.ds(pl.multiple_of(j * edge, edge), edge), :], sem_b.at[j])

    def place_tile(t, j):
        o = owner[t]
        n = count[o]
        count[o] = n + 1
        pair = occ[t] * CV_DEV + vir[t] + 1
        here = j - base

        @pl.when(n == 0)
        def _():
            first(t, o).start()
            head[0, o] = pair.astype(f32)

        @pl.when(n > 0)
        def _():
            head[0, o] = head[0, o] + ((pair << SHIFT) + (j << (2 * SHIFT))).astype(f32)

        @pl.when((n > 0) & (here >= 0) & (here < per_round))
        def _():
            second(t, here).start()

        return j + (n > 0).astype(jnp.int32)

    total = jnp.int32(0)
    for i in range(PIECES):
        loads[i].wait()
        total = lax.fori_loop(i * piece, (i + 1) * piece, place_tile, total, unroll=4)
    copy = pltpu.make_async_copy(head, pay.at[pl.ds(per_round * edge, HEAD), :], sem_h)
    copy.start()

    for j in range(per_round):

        @pl.when(base + j < total)
        def _():
            second(0, j).wait()

    copy.wait()

    def settle(d, c):
        @pl.when(count[d] > 0)
        def _():
            first(0, d).wait()

        return c

    lax.fori_loop(0, devices, settle, 0, unroll=8)


def pack(rnd, owner, occ, vir, amp, devices, per_round):
    tiles, edge = amp.shape[:2]
    return pl.pallas_call(
        functools.partial(pack_kernel, tiles, devices, per_round),
        grid_spec=pltpu.PrefetchScalarGridSpec(
            num_scalar_prefetch=4,
            in_specs=[ANY],
            out_specs=[pl.BlockSpec(memory_space=pltpu.HBM), pl.BlockSpec(memory_space=pltpu.VMEM)],
            scratch_shapes=[
                pltpu.VMEM((tiles, edge, edge), f32),
                pltpu.SMEM((devices,), jnp.int32),
                pltpu.SMEM((HEAD, 128), f32),
                pltpu.SemaphoreType.DMA((PIECES,)),
                pltpu.SemaphoreType.DMA((devices,)),
                pltpu.SemaphoreType.DMA((per_round,)),
                pltpu.SemaphoreType.DMA,
            ],
        ),
        out_shape=[
            pltpu.HBM((devices, edge, edge), f32),
            jax.ShapeDtypeStruct((per_round * edge + HEAD, edge), f32),
        ],
        compiler_params=pltpu.CompilerParams(vmem_limit_bytes=room(amp.shape, (per_round * edge, edge))),
        name="pack",
    )(rnd, owner, occ, vir, amp)


def pick_kernel(layer, per_round, rnd, place, codes, *refs):
    line = refs[:NZ]
    outs = refs[NZ:]
    edge = line[0].shape[1]
    z, mine = place[0], place[1]
    for k in range(NZ):
        at = z ^ k
        head = line[k][pl.ds(per_round * edge, HEAD), :]
        for m in range(layer):
            code = codes[k, z * layer + (mine ^ m)]
            here = (code >> (2 * SHIFT)) - rnd[0] * per_round
            full = ((code >> SHIFT) & MASK) > 0

            @pl.when(full & (here >= 0) & (here < per_round))
            def _():
                rows = pl.ds(pl.multiple_of(here * edge, edge), edge)
                outs[m][pl.ds(pl.multiple_of(at * edge, edge), edge), :] = line[k][rows, :]

            outs[m][pl.ds(pl.multiple_of(NZ * edge + at * HEAD, HEAD), HEAD), :] = head


def pick(rnd, place, codes, arrays, layer, per_round):
    rows, edge = arrays[0].shape
    whole = pl.BlockSpec(memory_space=pltpu.VMEM)
    return pl.pallas_call(
        functools.partial(pick_kernel, layer, per_round),
        grid_spec=pltpu.PrefetchScalarGridSpec(
            num_scalar_prefetch=3,
            in_specs=[whole] * NZ,
            out_specs=[whole] * layer,
        ),
        out_shape=[jax.ShapeDtypeStruct((NZ * (edge + HEAD), edge), f32)] * layer,
        compiler_params=pltpu.CompilerParams(vmem_limit_bytes=room((NZ, rows, edge), (layer, NZ * (edge + HEAD), edge))),
        name="pick",
    )(rnd, place, codes, *arrays)


def overflow_round(rnd, place, pay, layer, per_round, tie):
    row = per_round * pay.shape[1]

    def along(k):
        return [(z * layer + i, (z ^ k) * layer + i) for z in range(NZ) for i in range(layer)]

    cross = lax.ppermute(pay, AXES, along(2))
    near = lax.ppermute(pay, AXES, along(1))
    cross, tie = lax.optimization_barrier((cross, tie))
    line = [pay, near, cross, lax.ppermute(cross, AXES, along(1))]
    codes = jnp.stack([a[row] for a in line]).astype(jnp.int32)
    parts = pick(rnd, place, codes, line, layer, per_round)
    got = [parts[0]]
    for m in range(1, layer):
        pairs = [(z * layer + i, z * layer + (i ^ m)) for z in range(NZ) for i in range(layer)]
        got.append(lax.ppermute(parts[m], AXES, pairs))
    return got, tie


def split_kernel(per_step, wide, source, both):
    edge = both.shape[1] // 2
    for c in range(per_step):
        for a in range(wide):
            x = source[pl.ds(c * edge * wide + a, edge, stride=wide), :]
            h = x.astype(bf16)
            both[c, :edge, a * edge : (a + 1) * edge] = h
            both[c, edge:, a * edge : (a + 1) * edge] = (x - h.astype(f32)).astype(bf16)


def split(integrals):
    rows, wide, edge = integrals.shape
    blocks = rows // edge
    per_step = 4
    return pl.pallas_call(
        functools.partial(split_kernel, per_step, wide),
        grid=(blocks // per_step,),
        in_specs=[pl.BlockSpec((per_step * edge * wide, edge), lambda i: (i, 0))],
        out_specs=pl.BlockSpec((per_step, 2 * edge, wide * edge), lambda i: (i, 0, 0)),
        out_shape=jax.ShapeDtypeStruct((blocks, 2 * edge, wide * edge), bf16),
        compiler_params=pltpu.CompilerParams(vmem_limit_bytes=16 << 20),
        cost_estimate=pl.CostEstimate(flops=0, bytes_accessed=2 * rows * wide * edge * 4, transcendentals=0),
        name="split",
    )(integrals.reshape(rows * wide, edge))


def product_kernel(layer, firsts, low_occ, occs, per_round, cols, own, rnd, place, table, *refs):
    sources, refs = refs[:layer], refs[layer:]
    if firsts:
        first, refs = refs[0], refs[1:]
    both, keep, give, tiles, held, acc, queue, sem_t, sem_b, sem_o = refs
    edge = both.shape[1] // 2
    wide = acc.shape[0]
    count = layer * NZ
    z, mine, x, core = place[0], place[1], place[2], place[3]
    dot = functools.partial(jnp.dot, preferred_element_type=f32)

    slots = held.shape[0]

    def enter(base, n, where, number, ok):
        pair = number - 1
        p = pair >> CV_BITS
        queue[3 * (base + n)] = where
        queue[3 * (base + n) + 1] = p - low_occ
        queue[3 * (base + n) + 2] = pair & (CV_DEV - 1)
        ok = ok & (number > 0) & (p >= low_occ) & (p < low_occ + occs)
        return ok, n + ok.astype(jnp.int32)

    def pad(n):
        for u in range(3 * GROUP):
            queue[3 * n + u] = 0

    def fetch(g, u):
        slot = lax.rem(g, slots)
        return pltpu.make_async_copy(both.at[queue[3 * (g * GROUP + u) + 2]], held.at[slot, u], sem_b.at[slot, u])

    def ahead(g, groups):
        @pl.when(g < groups)
        def _():
            for u in range(GROUP):
                fetch(g, u).start()

    def work(ref, low, high, base, total, groups):
        def step(g, c):
            ahead(g + slots - 1, groups)
            for u in range(GROUP):
                fetch(g, u).wait()
            for u in range(GROUP):
                n = g * GROUP + u
                a = jnp.where(n - base < total, ref[queue[3 * n]], 0.0)
                ah = a.astype(bf16)
                al = (a - ah.astype(f32)).astype(bf16)
                b = held.at[lax.rem(g, slots), u]
                r = dot(jnp.concatenate([ah, ah], axis=1), b[...]) + dot(al, b[:edge, :])
                at = pl.ds(pl.multiple_of(queue[3 * n + 1] * edge, edge), edge)
                for k in range(wide):
                    acc[k, at, :] += r[:, k * edge : (k + 1) * edge]
            return c

        lax.fori_loop(low, high, step, 0)

    total = jnp.int32(0)
    if firsts:

        def listing(i, n):
            m, at = i // NZ, i % NZ
            return enter(0, n, at * layer + (mine ^ m), table[i] & MASK, True)[1]

        total = lax.fori_loop(0, count, listing, total, unroll=4)
        pad(total)
    early = (total + GROUP - 1) // GROUP
    for g in range(slots - 1):
        ahead(jnp.int32(g), early)

    seconds = jnp.int32(0)
    for m in range(layer):
        for k in range(NZ):
            code = table[m * NZ + k]
            here = (code >> (2 * SHIFT)) - rnd[0] * per_round
            ok, more = enter(GROUP * early, seconds, seconds, (code >> SHIFT) & MASK, (here >= 0) & (here < per_round))

            @pl.when(ok)
            def _():
                pltpu.make_async_copy(sources[m].at[pl.ds(k * edge, edge), :], tiles.at[seconds], sem_t.at[seconds]).start()

            seconds = more
    pad(GROUP * early + seconds)
    groups = early + (seconds + GROUP - 1) // GROUP
    for g in range(slots - 1):

        @pl.when(g >= early)
        def _():
            ahead(jnp.int32(g), groups)

    acc[...] = jnp.zeros_like(acc)
    if firsts:
        work(first, 0, early, 0, total, groups)

    def arrive(n, c):
        pltpu.make_async_copy(sources[0].at[pl.ds(0, edge), :], tiles.at[n], sem_t.at[n]).wait()
        return c

    lax.fori_loop(0, seconds, arrive, 0)
    work(tiles, early, groups, GROUP * early, seconds, groups)

    chips = cols // 2
    stores = []
    for part, out in enumerate((keep, give)):
        for j in range(chips):
            block = (lax.rem(x + j, chips) * 2 + (core ^ part)) * own
            stores.append(pltpu.make_async_copy(acc.at[pl.ds(block, own)], out.at[j], sem_o.at[part * chips + j]))
    for store in stores:
        store.start()
    for store in stores:
        store.wait()


def product(rnd, place, table, second, first, both, layer, per_round, cols, own, low_occ, occs):
    edge = both.shape[1] // 2
    wide = both.shape[2] // edge
    rows = occs * edge
    chips = cols // 2
    count = layer * NZ
    firsts = first is not None
    operands = [pltpu.with_memory_space_constraint(a, pltpu.HBM) for a in second]
    if firsts:
        operands.append(pltpu.with_memory_space_constraint(first, pltpu.VMEM))
    out = jax.ShapeDtypeStruct((chips, own, rows, edge), f32)
    return pl.pallas_call(
        functools.partial(product_kernel, layer, firsts, low_occ, occs, per_round, cols, own),
        grid_spec=pltpu.PrefetchScalarGridSpec(
            num_scalar_prefetch=3,
            in_specs=[ANY] * len(second) + [pl.BlockSpec(memory_space=pltpu.VMEM)] * firsts + [ANY],
            out_specs=[ANY, ANY],
            scratch_shapes=[
                pltpu.VMEM((count, edge, edge), f32),
                pltpu.VMEM((SLOTS, GROUP, 2 * edge, wide * edge), bf16),
                pltpu.VMEM((wide, rows, edge), f32),
                pltpu.SMEM((6 * (count + GROUP),), jnp.int32),
                pltpu.SemaphoreType.DMA((count,)),
                pltpu.SemaphoreType.DMA((SLOTS, GROUP)),
                pltpu.SemaphoreType.DMA((2 * chips,)),
            ],
        ),
        out_shape=[out, out],
        compiler_params=pltpu.CompilerParams(vmem_limit_bytes=room((count, edge, edge), (SLOTS * GROUP, edge, wide * edge), (wide, rows, edge), (GROUP, edge, 2 * wide * edge))),
        cost_estimate=pl.CostEstimate(flops=4 * count * edge * edge * edge * wide, bytes_accessed=16 << 20, transcendentals=0),
        name="product",
    )(rnd, place, table, *operands, both)


def chip_sum(keep, give, cols):
    got = lax.ppermute(give, "col", [(c, c ^ 1) for c in range(cols)])
    return [keep[j] + got[j] for j in range(cols // 2)]


def exchange(sums, cols):
    chips = cols // 2
    return [lax.ppermute(sums[j], "col", [(c, (c // 2 + j) % chips * 2 + c % 2) for c in range(cols)]) for j in range(1, chips)]


def body(amplitudes, amp_owner, amp_occ, amp_vir, integrals):
    rows, cols = lax.axis_size("row"), lax.axis_size("col")
    devices = rows * cols
    layer = devices // NZ
    per_round = max(1, amplitudes.shape[0] // 8)
    own = integrals.shape[1] // cols
    edge = amplitudes.shape[1]
    row, col = lax.axis_index("row"), lax.axis_index("col")
    me = row * cols + col
    place = jnp.stack([me // layer, me % layer, col // 2, col % 2]).astype(jnp.int32)
    owner = amp_owner[:, 0]

    def packed(r):
        return pack(r, owner, amp_occ, amp_vir, amplitudes, devices, per_round)

    zero = jnp.zeros((1,), jnp.int32)
    send, pay = packed(zero)
    first = lax.all_to_all(send, AXES, split_axis=0, concat_axis=0, tiled=True)
    got, both = overflow_round(zero, place, pay, layer, per_round, split(integrals))
    heads = jnp.stack([g[NZ * edge :].reshape(NZ, HEAD, 128)[:, 0] for g in got]).astype(jnp.int32)
    table = lax.dynamic_index_in_dim(heads, me, 2, keepdims=False).reshape(-1)
    most = jnp.max(jnp.sum(((heads >> SHIFT) & MASK) > 0, axis=2, dtype=jnp.int32))
    rounds = (most + per_round - 1) // per_round

    def run(r, table, second, firsts, low_occ, occs):
        return product(r, place, table, second, firsts, both, layer, per_round, cols, own, low_occ, occs)

    pieces, moved = [], None
    for g, occs in enumerate(SPANS):
        keep, give = run(zero, table, got, first, sum(SPANS[:g]), occs)
        if moved is not None:
            give, moved = lax.optimization_barrier((give, moved))
            pieces.append(functools.reduce(jnp.add, moved, sums[0]))
        sums = chip_sum(keep, give, cols)
        sums, table = lax.optimization_barrier((sums, table))
        moved = exchange(sums, cols)
    pieces.append(functools.reduce(jnp.add, moved, sums[0]))
    out = jnp.concatenate(pieces, axis=1)

    def more(carry):
        r, total = carry
        at = jnp.reshape(r, (1,))
        again, _ = overflow_round(at, place, packed(at)[1], layer, per_round, place)
        sums = chip_sum(*run(at, table, again, None, 0, OCC_DEV), cols)
        return r + 1, functools.reduce(jnp.add, exchange(sums, cols), total + sums[0])

    return lax.while_loop(lambda c: c[0] < rounds, more, (jnp.int32(1), out))[1]


def solution(mesh):
    in_specs = (
        P(("row", "col"), None, None),
        P(("row", "col"), None),
        P(("row", "col")),
        P(("row", "col")),
        P("col", None, None),
    )
    out_specs = P("col", "row", None)
    return jax.shard_map(body, mesh=mesh, in_specs=in_specs, out_specs=out_specs, check_vma=False)
```

time: 243 us -> 113 us (0.47)
  waiting for transfers between devices: 130 us -> 57.9 us
  matrix products: 46.1 us -> 0 us
  Pallas kernels: 0 us -> 26.4 us
  local copies, waits for them, and re-layouts: 23.2 us -> 4.5 us
  other arithmetic: 16.6 us -> 2.07 us
  between operations: 13.5 us -> 1.02 us
  starting transfers between devices: 13.4 us -> 21.5 us
    all_to_all x2 -> x1, waiting for transfers between devices: 92.5 us -> 0.01 us  [body(): first = lax.all_to_all(send, AXES, split_axis=0, concat_axis=0, tiled=True)]
    ppermute x0 -> x14, waiting for transfers between devices: none -> 57.9 us  [the longest x7 38.9 us: overflow_round(): got.append(lax.ppermute(parts[m], AXES, pairs))]
    dot_general x1 -> x0, matrix products: 46.1 us -> none  [body(): jnp.einsum('pcij,cjak->apik', grid, blocks, precision=lax.Precision.HIGHEST)]
    reduce_scatter x1 -> x0, waiting for transfers between devices: 37.2 us -> none  [body(): lax.psum_scatter(result.reshape(own_tiles * lax.axis_size('col'), OCC_DEV...]
    pallas_call x0 -> x5, Pallas kernels: none -> 26.4 us  [the longest x2 16.5 us: product(): pl.pallas_call(functools.partial(product_kernel, layer, firsts, low_occ,...]
    ppermute x0 -> x14, starting transfers between devices: none -> 15.9 us  [the longest x7 9.31 us: overflow_round(): got.append(lax.ppermute(parts[m], AXES, pairs))]
    broadcast_in_dim x2 -> x0, local copies, waits for them, and re-layouts: 14 us -> none  [the longest x1 11.5 us: body(): jnp.zeros((OCC_DEV * CV_DEV, tile, tile), jnp.float32).at[got_pairs]]
    scatter-add x1 -> x0, other arithmetic: 13.6 us -> none  [body(): jnp.zeros((OCC_DEV * CV_DEV, tile, tile), jnp.float32).at[got_pairs]]
  transfers between devices with their start and end apart: 3 -> 15, of which waited for: 2 -> 9; matrix products, arithmetic and copies ran while one was open for 4% -> 1% of each run, Pallas kernels for 0% -> 14%
where the time goes in v1:
time: 113 us
  waiting for transfers between devices  57.9 us (51%)
  Pallas kernels  26.4 us (23%)
  starting transfers between devices  21.5 us (19%)
  local copies, waits for them, and re-layouts  4.5 us (4%)
  other arithmetic  2.07 us (2%)
    ppermute x7, waiting for transfers between devices, overflow_round(): got.append(lax.ppermute(parts[m], AXES, pairs))  38.9 us
    pallas_call x2, Pallas kernels, product(): pl.pallas_call(functools.partial(product_kernel, layer, firsts, low_occ,...  16.5 us
    ppermute x2, waiting for transfers between devices, exchange(): lax.ppermute(sums[j], 'col', [(c, (c // 2 + j) % chips * 2 + c % 2) for c...  10.9 us
    ppermute x7, starting transfers between devices, overflow_round(): got.append(lax.ppermute(parts[m], AXES, pairs))  9.31 us
    all_to_all x1, starting transfers between devices, body(): first = lax.all_to_all(send, AXES, split_axis=0, concat_axis=0, tiled=True)  5.51 us
    pallas_call x1, Pallas kernels, split(): pl.pallas_call(functools.partial(split_kernel, per_step, wide), grid=(blo...  5.06 us
    ppermute x2, waiting for transfers between devices, chip_sum(): got = lax.ppermute(give, 'col', [(c, c ^ 1) for c in range(cols)])  4.54 us
    unnamed x24, local copies, waits for them, and re-layouts  4.11 us
  transfers between devices with their start and end apart: 15, of which 9 were waited for; matrix products, arithmetic and copies ran while one was open for 1% of the time, Pallas kernels for 14%

profile of v1, /device:TPU:0, one launch (start us, length us, event | category | flops | bytes accessed | tf_op | source)
XLA Modules:
  0.0 113.3 jit_solution(3006631783118712193)
XLA Ops:
  0.0 3.8 %pack.2 = (f32[32,128,128]{2,1,0:T(8,128)}, f32[520,128]{1,0:T(8,128)S(1)}) custom-call(s32[1]{0:T(128)} %constant.67.clone.1.rnd, s32[32]{0:T(128)} %bitcast.80, s32[32]{0:T(128)} %occ.1, s32[32]{0:T(128)} %vir.1, f32[32,128,128]{2,1,0:T(8,128)} %amp.1), custom_call_target="tpu_custom_call" | custom-call | tf_op jit(solution)/shard_map/pack/pallas_call | solution.py:103
  3.8 4.0 %collective-permute-start.13 = (f32[520,128]{1,0:T(8,128)S(1)}, f32[520,128]{1,0:T(8,128)S(1)}, u32[]{:S(2)}, u32[]{:S(2)}) collective-permute-start(f32[520,128]{1,0:T(8,128)S(1)} %get-tuple-element.94.refs_0_), channel_id=1, source_target_pairs={{0,16},{1,17},{2,18},{3,19},{4,20},{5,21},{6,22},{7,23},{8,24},{9,... | collective-permute-start | bytes 798728 | tf_op jit(solution)/shard_map/ppermute | solution.py:171
  7.8 1.6 %collective-permute-start.12 = (f32[520,128]{1,0:T(8,128)S(1)}, f32[520,128]{1,0:T(8,128)S(1)}, u32[]{:S(2)}, u32[]{:S(2)}) collective-permute-start(f32[520,128]{1,0:T(8,128)S(1)} %get-tuple-element.94.refs_0_), channel_id=1, source_target_pairs={{0,8},{1,9},{2,10},{3,11},{4,12},{5,13},{6,14},{7,15},{8,0},{9,1},... | collective-permute-start | bytes 798728 | tf_op jit(solution)/shard_map/ppermute | solution.py:172
  9.4 3.4 %copy-done = f32[4096,4,128]{2,1,0:T(4,128)S(1)} copy-done((f32[4096,4,128]{2,1,0:T(4,128)S(1)}, f32[4096,4,128]{2,1,0:T(4,128)}, u32[]{:S(2)}) %copy-start) | copy-done | bytes 8388632
  12.8 5.1 %split.1.refs_9_ = bf16[32,256,512]{2,1,0:T(8,128)(2,1)} custom-call(f32[16384,128]{1,0:T(8,128)S(1)} %bitcast.79), custom_call_target="tpu_custom_call" | custom-call | bytes 16777216 | tf_op jit(solution)/shard_map/split/pallas_call | solution.py:198
  17.8 2.3 %collective-permute-done.13.refs_2_ = f32[520,128]{1,0:T(8,128)S(1)} collective-permute-done((f32[520,128]{1,0:T(8,128)S(1)}, f32[520,128]{1,0:T(8,128)S(1)}, u32[]{:S(2)}, u32[]{:S(2)}) %collective-permute-start.13) | collective-permute-done | bytes 266272 | tf_op jit(solution)/shard_map/ppermute | solution.py:171
  20.7 5.5 %all-to-all-start = ((f32[32,128,128]{2,1,0:T(8,128)}), f32[32,128,128]{2,1,0:T(8,128)S(1)}, u32[]{:S(2)}, u32[]{:S(2)}) async-start(f32[32,128,128]{2,1,0:T(8,128)} %get-tuple-element.104), calls=%async_computation | async-start | bytes 4194304 | tf_op jit(solution)/shard_map/all_to_all | solution.py:382
  26.4 1.3 %collective-permute-done.14.refs_3_ = f32[520,128]{1,0:T(8,128)S(1)} collective-permute-done((f32[520,128]{1,0:T(8,128)S(1)}, f32[520,128]{1,0:T(8,128)S(1)}, u32[]{:S(2)}, u32[]{:S(2)}) %collective-permute-start.14) | collective-permute-done | bytes 266272 | tf_op jit(solution)/shard_map/ppermute | solution.py:174
  27.7 1.1 pick.2
  29.1 0.9 collective-permute-start.18
  30.0 1.3 %collective-permute-start.17 = (f32[544,128]{1,0:T(8,128)S(1)}, f32[544,128]{1,0:T(8,128)S(1)}, u32[]{:S(2)}, u32[]{:S(2)}) collective-permute-start(f32[544,128]{1,0:T(8,128)S(1)} %get-tuple-element.99), channel_id=1, source_target_pairs={{0,3},{1,2},{2,1},{3,0},{4,7},{5,6},{6,5},{7,4},{8,11},{9,10},{10,... | collective-permute-start | bytes 835592 | tf_op jit(solution)/shard_map/ppermute | solution.py:180
  31.3 1.0 collective-permute-start.16
  32.4 16.8 %collective-permute-done.19.refs_5_ = f32[544,128]{1,0:T(8,128)S(1)} collective-permute-done((f32[544,128]{1,0:T(8,128)S(1)}, f32[544,128]{1,0:T(8,128)S(1)}, u32[]{:S(2)}, u32[]{:S(2)}) %collective-permute-start.19) | collective-permute-done | bytes 278560 | tf_op jit(solution)/shard_map/ppermute | solution.py:180
  49.2 4.5 %collective-permute-start.21 = (f32[544,128]{1,0:T(8,128)S(1)}, f32[544,128]{1,0:T(8,128)S(1)}, u32[]{:S(2)}, u32[]{:S(2)}) collective-permute-start(f32[544,128]{1,0:T(8,128)S(1)} %get-tuple-element.103), channel_id=1, source_target_pairs={{0,7},{1,6},{2,5},{3,4},{4,3},{5,2},{6,1},{7,0},{8,15},{9,14},{10,... | collective-permute-start | bytes 835592 | tf_op jit(solution)/shard_map/ppermute | solution.py:180
  53.6 6.3 %collective-permute-done.18.refs_4_ = f32[544,128]{1,0:T(8,128)S(1)} collective-permute-done((f32[544,128]{1,0:T(8,128)S(1)}, f32[544,128]{1,0:T(8,128)S(1)}, u32[]{:S(2)}, u32[]{:S(2)}) %collective-permute-start.18) | collective-permute-done | bytes 278560 | tf_op jit(solution)/shard_map/ppermute | solution.py:180
  60.0 1.3 %collective-permute-start.20 = (f32[544,128]{1,0:T(8,128)S(1)}, f32[544,128]{1,0:T(8,128)S(1)}, u32[]{:S(2)}, u32[]{:S(2)}) collective-permute-start(f32[544,128]{1,0:T(8,128)S(1)} %get-tuple-element.102), channel_id=1, source_target_pairs={{0,6},{1,7},{2,4},{3,5},{4,2},{5,3},{6,0},{7,1},{8,14},{9,15},{10,... | collective-permute-start | bytes 835592 | tf_op jit(solution)/shard_map/ppermute | solution.py:180
  61.4 6.6 %collective-permute-done.21.refs_7_ = f32[544,128]{1,0:T(8,128)S(1)} collective-permute-done((f32[544,128]{1,0:T(8,128)S(1)}, f32[544,128]{1,0:T(8,128)S(1)}, u32[]{:S(2)}, u32[]{:S(2)}) %collective-permute-start.21) | collective-permute-done | bytes 278560 | tf_op jit(solution)/shard_map/ppermute | solution.py:180
  68.0 9.1 %collective-permute-done.20.refs_6_ = f32[544,128]{1,0:T(8,128)S(1)} collective-permute-done((f32[544,128]{1,0:T(8,128)S(1)}, f32[544,128]{1,0:T(8,128)S(1)}, u32[]{:S(2)}, u32[]{:S(2)}) %collective-permute-start.20) | collective-permute-done | bytes 278560 | tf_op jit(solution)/shard_map/ppermute | solution.py:180
  78.2 6.7 %product.3 = (f32[2,1,640,128]{3,2,1,0:T(8,128)S(1)}, f32[2,1,640,128]{3,2,1,0:T(8,128)S(1)}) custom-call(s32[1]{0:T(128)} %constant.67.clone.1.rnd, s32[4]{0:T(128)S(1)} %pad_add_fusion.place, s32[32]{0:T(128)S(1)} %reshape.169.table, f32[544,128]{1,0:T(8,128)} %copy-done.2, f32[544,128]{1,0:T(8,128)} %copy-done.14, f32[544,128]{1,0:T(8,128)} %copy-done.13, ...), custom_call_target="tpu_custom_call" | custom-call | flops 1073741824 | bytes 16777216 | tf_op jit(solution)/shard_map/product/pallas_call | solution.py:332
  84.9 2.1 %collective-permute-done.22 = f32[2,1,640,128]{3,2,1,0:T(8,128)S(1)} collective-permute-done((f32[2,1,640,128]{3,2,1,0:T(8,128)S(1)}, f32[2,1,640,128]{3,2,1,0:T(8,128)S(1)}, u32[]{:S(2)}, u32[]{:S(2)}) %collective-permute-start.22) | collective-permute-done | bytes 655392 | tf_op jit(solution)/shard_map/ppermute | solution.py:356
  87.2 9.8 %product.4 = (f32[2,1,896,128]{3,2,1,0:T(8,128)S(1)}, f32[2,1,896,128]{3,2,1,0:T(8,128)S(1)}) custom-call(s32[1]{0:T(128)} %constant.67.clone.1.rnd, s32[4]{0:T(128)S(1)} %pad_add_fusion.place, s32[32]{0:T(128)S(1)} %reshape.169.table, f32[544,128]{1,0:T(8,128)} %copy-done.2, f32[544,128]{1,0:T(8,128)} %copy-done.14, f32[544,128]{1,0:T(8,128)} %copy-done.13, ...), custom_call_target="tpu_custom_call" | custom-call | flops 1073741824 | bytes 16777216 | tf_op jit(solution)/shard_map/product/pallas_call | solution.py:332
  97.1 2.5 %collective-permute-done.24 = f32[2,1,896,128]{3,2,1,0:T(8,128)S(1)} collective-permute-done((f32[2,1,896,128]{3,2,1,0:T(8,128)S(1)}, f32[2,1,896,128]{3,2,1,0:T(8,128)S(1)}, u32[]{:S(2)}, u32[]{:S(2)}) %collective-permute-start.24) | collective-permute-done | bytes 917536 | tf_op jit(solution)/shard_map/ppermute | solution.py:356
  101.4 10.9 %collective-permute-done.25 = f32[1,896,128]{2,1,0:T(8,128)S(1)} collective-permute-done((f32[1,896,128]{2,1,0:T(8,128)S(1)}, f32[1,896,128]{2,1,0:T(8,128)S(1)}, u32[]{:S(2)}, u32[]{:S(2)}) %collective-permute-start.25) | collective-permute-done | bytes 458784 | tf_op jit(solution)/shard_map/ppermute | solution.py:362
  112.3 0.9 pad_maximum_fusion
  (70 shorter events, 3.6 us)
Async XLA Ops:
  3.8 16.3 %collective-permute-start.13 = (f32[520,128]{1,0:T(8,128)S(1)}, f32[520,128]{1,0:T(8,128)S(1)}, u32[]{:S(2)}, u32[]{:S(2)}) collective-permute-start(f32[520,128]{1,0:T(8,128)S(1)} %get-tuple-element.94.refs_0_), channel_id=1, source_target_pairs={{0,16},{1,17},{2,18},{3,19},{4,20},{5,21},{6,22},{7,23},{8,24},{9,... | collective-permute-start | bytes 798728 | tf_op jit(solution)/shard_map/ppermute | solution.py:171
  7.8 18.6 %collective-permute-start.12 = (f32[520,128]{1,0:T(8,128)S(1)}, f32[520,128]{1,0:T(8,128)S(1)}, u32[]{:S(2)}, u32[]{:S(2)}) collective-permute-start(f32[520,128]{1,0:T(8,128)S(1)} %get-tuple-element.94.refs_0_), channel_id=1, source_target_pairs={{0,8},{1,9},{2,10},{3,11},{4,12},{5,13},{6,14},{7,15},{8,0},{9,1},... | collective-permute-start | bytes 798728 | tf_op jit(solution)/shard_map/ppermute | solution.py:172
  20.1 7.6 %collective-permute-start.14 = (f32[520,128]{1,0:T(8,128)S(1)}, f32[520,128]{1,0:T(8,128)S(1)}, u32[]{:S(2)}, u32[]{:S(2)}) collective-permute-start(f32[520,128]{1,0:T(8,128)S(1)} %collective-permute-done.13.refs_2_), channel_id=1, source_target_pairs={{0,8},{1,9},{2,10},{3,11},{4,12},{5,13},{6,14},{7,15},{8,0},{9,1},... | collective-permute-start | bytes 798728 | tf_op jit(solution)/shard_map/ppermute | solution.py:174
  20.7 57.5 %all-to-all-start = ((f32[32,128,128]{2,1,0:T(8,128)}), f32[32,128,128]{2,1,0:T(8,128)S(1)}, u32[]{:S(2)}, u32[]{:S(2)}) async-start(f32[32,128,128]{2,1,0:T(8,128)} %get-tuple-element.104), calls=%async_computation | async-start | bytes 4194304 | tf_op jit(solution)/shard_map/all_to_all | solution.py:382
  28.8 49.4 %copy-start.2 = (f32[544,128]{1,0:T(8,128)}, f32[544,128]{1,0:T(8,128)S(1)}, u32[]{:S(2)}) copy-start(f32[544,128]{1,0:T(8,128)S(1)} %get-tuple-element.96.refs_0_) | copy-start | bytes 835588
  28.8 20.4 %collective-permute-start.19 = (f32[544,128]{1,0:T(8,128)S(1)}, f32[544,128]{1,0:T(8,128)S(1)}, u32[]{:S(2)}, u32[]{:S(2)}) collective-permute-start(f32[544,128]{1,0:T(8,128)S(1)} %get-tuple-element.101), channel_id=1, source_target_pairs={{0,5},{1,4},{2,7},{3,6},{4,1},{5,0},{6,3},{7,2},{8,13},{9,12},{10,... | collective-permute-start | bytes 835592 | tf_op jit(solution)/shard_map/ppermute | solution.py:180
  29.1 30.9 %collective-permute-start.18 = (f32[544,128]{1,0:T(8,128)S(1)}, f32[544,128]{1,0:T(8,128)S(1)}, u32[]{:S(2)}, u32[]{:S(2)}) collective-permute-start(f32[544,128]{1,0:T(8,128)S(1)} %get-tuple-element.100), channel_id=1, source_target_pairs={{0,4},{1,5},{2,6},{3,7},{4,0},{5,1},{6,2},{7,3},{8,12},{9,13},{10,... | collective-permute-start | bytes 835592 | tf_op jit(solution)/shard_map/ppermute | solution.py:180
  30.0 31.2 %collective-permute-start.17 = (f32[544,128]{1,0:T(8,128)S(1)}, f32[544,128]{1,0:T(8,128)S(1)}, u32[]{:S(2)}, u32[]{:S(2)}) collective-permute-start(f32[544,128]{1,0:T(8,128)S(1)} %get-tuple-element.99), channel_id=1, source_target_pairs={{0,3},{1,2},{2,1},{3,0},{4,7},{5,6},{6,5},{7,4},{8,11},{9,10},{10,... | collective-permute-start | bytes 835592 | tf_op jit(solution)/shard_map/ppermute | solution.py:180
  31.3 29.9 %collective-permute-start.16 = (f32[544,128]{1,0:T(8,128)S(1)}, f32[544,128]{1,0:T(8,128)S(1)}, u32[]{:S(2)}, u32[]{:S(2)}) collective-permute-start(f32[544,128]{1,0:T(8,128)S(1)} %get-tuple-element.98), channel_id=1, source_target_pairs={{0,2},{1,3},{2,0},{3,1},{4,6},{5,7},{6,4},{7,5},{8,10},{9,11},{10,... | collective-permute-start | bytes 835592 | tf_op jit(solution)/shard_map/ppermute | solution.py:180
  32.3 29.0 %collective-permute-start.15 = (f32[544,128]{1,0:T(8,128)S(1)}, f32[544,128]{1,0:T(8,128)S(1)}, u32[]{:S(2)}, u32[]{:S(2)}) collective-permute-start(f32[544,128]{1,0:T(8,128)S(1)} %get-tuple-element.97), channel_id=1, source_target_pairs={{0,1},{1,0},{2,3},{3,2},{4,5},{5,4},{6,7},{7,6},{8,9},{9,8},{10,11... | collective-permute-start | bytes 835592 | tf_op jit(solution)/shard_map/ppermute | solution.py:180
  49.1 29.0 %copy-start.10 = (f32[544,128]{1,0:T(8,128)}, f32[544,128]{1,0:T(8,128)S(1)}, u32[]{:S(2)}) copy-start(f32[544,128]{1,0:T(8,128)S(1)} %collective-permute-done.19.refs_5_) | copy-start | bytes 835588
  49.2 18.8 %collective-permute-start.21 = (f32[544,128]{1,0:T(8,128)S(1)}, f32[544,128]{1,0:T(8,128)S(1)}, u32[]{:S(2)}, u32[]{:S(2)}) collective-permute-start(f32[544,128]{1,0:T(8,128)S(1)} %get-tuple-element.103), channel_id=1, source_target_pairs={{0,7},{1,6},{2,5},{3,4},{4,3},{5,2},{6,1},{7,0},{8,15},{9,14},{10,... | collective-permute-start | bytes 835592 | tf_op jit(solution)/shard_map/ppermute | solution.py:180
  60.0 18.2 %copy-start.11 = (f32[544,128]{1,0:T(8,128)}, f32[544,128]{1,0:T(8,128)S(1)}, u32[]{:S(2)}) copy-start(f32[544,128]{1,0:T(8,128)S(1)} %collective-permute-done.18.refs_4_) | copy-start | bytes 835588
  60.0 17.1 %collective-permute-start.20 = (f32[544,128]{1,0:T(8,128)S(1)}, f32[544,128]{1,0:T(8,128)S(1)}, u32[]{:S(2)}, u32[]{:S(2)}) collective-permute-start(f32[544,128]{1,0:T(8,128)S(1)} %get-tuple-element.102), channel_id=1, source_target_pairs={{0,6},{1,7},{2,4},{3,5},{4,2},{5,3},{6,0},{7,1},{8,14},{9,15},{10,... | collective-permute-start | bytes 835592 | tf_op jit(solution)/shard_map/ppermute | solution.py:180
  61.3 16.9 %copy-start.12 = (f32[544,128]{1,0:T(8,128)}, f32[544,128]{1,0:T(8,128)S(1)}, u32[]{:S(2)}) copy-start(f32[544,128]{1,0:T(8,128)S(1)} %collective-permute-done.17.refs_3_) | copy-start | bytes 835588
  61.3 15.8 %copy-start.13 = (f32[544,128]{1,0:T(8,128)}, f32[544,128]{1,0:T(8,128)S(1)}, u32[]{:S(2)}) copy-start(f32[544,128]{1,0:T(8,128)S(1)} %collective-permute-done.16.refs_2_) | copy-start | bytes 835588
  61.3 15.8 %copy-start.14 = (f32[544,128]{1,0:T(8,128)}, f32[544,128]{1,0:T(8,128)S(1)}, u32[]{:S(2)}) copy-start(f32[544,128]{1,0:T(8,128)S(1)} %collective-permute-done.15.refs_1_) | copy-start | bytes 835588
  84.9 2.2 %collective-permute-start.22 = (f32[2,1,640,128]{3,2,1,0:T(8,128)S(1)}, f32[2,1,640,128]{3,2,1,0:T(8,128)S(1)}, u32[]{:S(2)}, u32[]{:S(2)}) collective-permute-start(f32[2,1,640,128]{3,2,1,0:T(8,128)S(1)} %get-tuple-element.107), channel_id=1, source_target_pairs={{0,1},{1,0},{2,3},{3,2},{4,5},{5,4},{6,7},{7,6},{8,9},{9,8},{10,11... | collective-permute-start | bytes 1966088 | tf_op jit(solution)/shard_map/ppermute | solution.py:356
  87.1 9.9 %collective-permute-start.23 = (f32[1,640,128]{2,1,0:T(8,128)S(1)}, f32[1,640,128]{2,1,0:T(8,128)S(1)}, u32[]{:S(2)}, u32[]{:S(2)}) collective-permute-start(f32[1,640,128]{2,1,0:T(8,128)S(1)} %get-tuple-element.111), channel_id=1, source_target_pairs={{0,2},{1,3},{2,0},{3,1},{4,6},{5,7},{6,4},{7,5},{8,10},{9,11},{10,... | collective-permute-start | bytes 983048 | tf_op jit(solution)/shard_map/ppermute | solution.py:362
  97.0 2.5 %collective-permute-start.24 = (f32[2,1,896,128]{3,2,1,0:T(8,128)S(1)}, f32[2,1,896,128]{3,2,1,0:T(8,128)S(1)}, u32[]{:S(2)}, u32[]{:S(2)}) collective-permute-start(f32[2,1,896,128]{3,2,1,0:T(8,128)S(1)} %get-tuple-element.114), channel_id=1, source_target_pairs={{0,1},{1,0},{2,3},{3,2},{4,5},{5,4},{6,7},{7,6},{8,9},{9,8},{10,11... | collective-permute-start | bytes 2752520 | tf_op jit(solution)/shard_map/ppermute | solution.py:356
  99.7 12.6 %collective-permute-start.25 = (f32[1,896,128]{2,1,0:T(8,128)S(1)}, f32[1,896,128]{2,1,0:T(8,128)S(1)}, u32[]{:S(2)}, u32[]{:S(2)}) collective-permute-start(f32[1,896,128]{2,1,0:T(8,128)S(1)} %get-tuple-element.116), channel_id=1, source_target_pairs={{0,2},{1,3},{2,0},{3,1},{4,6},{5,7},{6,4},{7,5},{8,10},{9,11},{10,... | collective-permute-start | bytes 1376264 | tf_op jit(solution)/shard_map/ppermute | solution.py:362
  101.3 11.9 %copy-start.17 = (s32[32,1]{0,1:T(1,128)S(1)}, s32[32,1]{0,1:T(1,128)}, u32[]{:S(2)}) copy-start(s32[32,1]{0,1:T(1,128)} %param.8) | copy-start | bytes 388
  101.4 11.9 %copy-start.18 = (s32[32]{0:T(128)S(1)}, s32[32]{0:T(128)}, u32[]{:S(2)}) copy-start(s32[32]{0:T(128)} %occ.1) | copy-start | bytes 388
  101.4 11.9 %copy-start.19 = (s32[32]{0:T(128)S(1)}, s32[32]{0:T(128)}, u32[]{:S(2)}) copy-start(s32[32]{0:T(128)} %vir.1) | copy-start | bytes 388
  (3 other events, 13.3 us)

commit v2 on v1

--- a/solution.py
+++ b/solution.py
@@ -181,41 +181,52 @@
     return got, tie
 
 
-def split_kernel(per_step, wide, source, both):
+def block_order(place, wide, cols):
+    chips, own = cols // 2, wide // cols
+    x, core = place[2], place[3]
+    return [(lax.rem(x + j, chips) * 2 + (core ^ part)) * own + o for part in range(2) for j in range(chips) for o in range(own)]
+
+
+def split_kernel(per_step, wide, cols, place, source, both):
     edge = both.shape[1] // 2
+    order = block_order(place, wide, cols)
     for c in range(per_step):
         for a in range(wide):
-            x = source[pl.ds(c * edge * wide + a, edge, stride=wide), :]
+            x = source[pl.ds(c * edge * wide + order[a], edge, stride=wide), :]
             h = x.astype(bf16)
             both[c, :edge, a * edge : (a + 1) * edge] = h
             both[c, edge:, a * edge : (a + 1) * edge] = (x - h.astype(f32)).astype(bf16)
 
 
-def split(integrals):
+def split(place, integrals, cols):
     rows, wide, edge = integrals.shape
     blocks = rows // edge
     per_step = 4
     return pl.pallas_call(
-        functools.partial(split_kernel, per_step, wide),
-        grid=(blocks // per_step,),
-        in_specs=[pl.BlockSpec((per_step * edge * wide, edge), lambda i: (i, 0))],
-        out_specs=pl.BlockSpec((per_step, 2 * edge, wide * edge), lambda i: (i, 0, 0)),
+        functools.partial(split_kernel, per_step, wide, cols),
+        grid_spec=pltpu.PrefetchScalarGridSpec(
+            num_scalar_prefetch=1,
+            grid=(blocks // per_step,),
+            in_specs=[pl.BlockSpec((per_step * edge * wide, edge), lambda i, at: (i, 0))],
+            out_specs=pl.BlockSpec((per_step, 2 * edge, wide * edge), lambda i, at: (i, 0, 0)),
+        ),
         out_shape=jax.ShapeDtypeStruct((blocks, 2 * edge, wide * edge), bf16),
         compiler_params=pltpu.CompilerParams(vmem_limit_bytes=16 << 20),
         cost_estimate=pl.CostEstimate(flops=0, bytes_accessed=2 * rows * wide * edge * 4, transcendentals=0),
         name="split",
-    )(integrals.reshape(rows * wide, edge))
+    )(place, integrals.reshape(rows * wide, edge))
 
 
 def product_kernel(layer, firsts, low_occ, occs, per_round, cols, own, rnd, place, table, *refs):
     sources, refs = refs[:layer], refs[layer:]
     if firsts:
         first, refs = refs[0], refs[1:]
-    both, keep, give, tiles, held, acc, queue, sem_t, sem_b, sem_o = refs
+    both, keep, give, tiles, held, queue, sem_t, sem_b = refs
     edge = both.shape[1] // 2
-    wide = acc.shape[0]
+    wide = both.shape[2] // edge
     count = layer * NZ
-    z, mine, x, core = place[0], place[1], place[2], place[3]
+    blocks = [(out, j, o) for out in (keep, give) for j in range(cols // 2) for o in range(own)]
+    mine = place[1]
     dot = functools.partial(jnp.dot, preferred_element_type=f32)
 
     slots = held.shape[0]
@@ -256,8 +267,8 @@
                 b = held.at[lax.rem(g, slots), u]
                 r = dot(jnp.concatenate([ah, ah], axis=1), b[...]) + dot(al, b[:edge, :])
                 at = pl.ds(pl.multiple_of(queue[3 * n + 1] * edge, edge), edge)
-                for k in range(wide):
-                    acc[k, at, :] += r[:, k * edge : (k + 1) * edge]
+                for k, (out, j, o) in enumerate(blocks):
+                    out[j, o, at, :] += r[:, k * edge : (k + 1) * edge]
             return c
 
         lax.fori_loop(low, high, step, 0)
@@ -295,7 +306,8 @@
         def _():
             ahead(jnp.int32(g), groups)
 
-    acc[...] = jnp.zeros_like(acc)
+    keep[...] = jnp.zeros_like(keep)
+    give[...] = jnp.zeros_like(give)
     if firsts:
         work(first, 0, early, 0, total, groups)
 
@@ -305,17 +317,6 @@
 
     lax.fori_loop(0, seconds, arrive, 0)
     work(tiles, early, groups, GROUP * early, seconds, groups)
-
-    chips = cols // 2
-    stores = []
-    for part, out in enumerate((keep, give)):
-        for j in range(chips):
-            block = (lax.rem(x + j, chips) * 2 + (core ^ part)) * own
-            stores.append(pltpu.make_async_copy(acc.at[pl.ds(block, own)], out.at[j], sem_o.at[part * chips + j]))
-    for store in stores:
-        store.start()
-    for store in stores:
-        store.wait()
 
 
 def product(rnd, place, table, second, first, both, layer, per_round, cols, own, low_occ, occs):
@@ -328,21 +329,19 @@
     operands = [pltpu.with_memory_space_constraint(a, pltpu.HBM) for a in second]
     if firsts:
         operands.append(pltpu.with_memory_space_constraint(first, pltpu.VMEM))
-    out = jax.ShapeDtypeStruct((chips, own, rows, edge), f32)
+    out = pltpu.VMEM((chips, own, rows, edge), f32)
     return pl.pallas_call(
         functools.partial(product_kernel, layer, firsts, low_occ, occs, per_round, cols, own),
         grid_spec=pltpu.PrefetchScalarGridSpec(
             num_scalar_prefetch=3,
             in_specs=[ANY] * len(second) + [pl.BlockSpec(memory_space=pltpu.VMEM)] * firsts + [ANY],
-            out_specs=[ANY, ANY],
+            out_specs=[pl.BlockSpec(memory_space=pltpu.VMEM)] * 2,
             scratch_shapes=[
                 pltpu.VMEM((count, edge, edge), f32),
                 pltpu.VMEM((SLOTS, GROUP, 2 * edge, wide * edge), bf16),
-                pltpu.VMEM((wide, rows, edge), f32),
                 pltpu.SMEM((6 * (count + GROUP),), jnp.int32),
                 pltpu.SemaphoreType.DMA((count,)),
                 pltpu.SemaphoreType.DMA((SLOTS, GROUP)),
-                pltpu.SemaphoreType.DMA((2 * chips,)),
             ],
         ),
         out_shape=[out, out],
@@ -380,7 +379,7 @@
     zero = jnp.zeros((1,), jnp.int32)
     send, pay = packed(zero)
     first = lax.all_to_all(send, AXES, split_axis=0, concat_axis=0, tiled=True)
-    got, both = overflow_round(zero, place, pay, layer, per_round, split(integrals))
+    got, both = overflow_round(zero, place, pay, layer, per_round, split(place, integrals, cols))
     heads = jnp.stack([g[NZ * edge :].reshape(NZ, HEAD, 128)[:, 0] for g in got]).astype(jnp.int32)
     table = lax.dynamic_index_in_dim(heads, me, 2, keepdims=False).reshape(-1)
     most = jnp.max(jnp.sum(((heads >> SHIFT) & MASK) > 0, axis=2, dtype=jnp.int32))

time: 113 us -> 112 us (level)
  Pallas kernels: 26.4 us -> 24.3 us
  waiting for transfers between devices: 57.9 us -> 59.4 us
    pallas_call x2, Pallas kernels: 16.5 us -> 13.8 us  [product(): pl.pallas_call(functools.partial(product_kernel, layer, firsts, low_occ,...]
    ppermute x2, waiting for transfers between devices: 10.9 us -> 13 us  [exchange(): lax.ppermute(sums[j], 'col', [(c, (c // 2 + j) % chips * 2 + c % 2) for c...]
  transfers between devices with their start and end apart: 15 -> 15, of which waited for: 9 -> 10; matrix products, arithmetic and copies ran while one was open for 1% -> 1% of each run, Pallas kernels for 14% -> 12%
where the time goes in v2:
time: 112 us; the launch traced here: 113 us
  waiting for transfers between devices  59.4 us (53%)
  Pallas kernels  24.3 us (22%)
  starting transfers between devices  21.7 us (19%)
  local copies, waits for them, and re-layouts  4.5 us (4%)
  other arithmetic  2.06 us (2%)
    ppermute x7, waiting for transfers between devices, overflow_round(): got.append(lax.ppermute(parts[m], AXES, pairs))  39.2 us
    pallas_call x2, Pallas kernels, product(): pl.pallas_call(functools.partial(product_kernel, layer, firsts, low_occ,...  13.8 us
    ppermute x2, waiting for transfers between devices, exchange(): lax.ppermute(sums[j], 'col', [(c, (c // 2 + j) % chips * 2 + c % 2) for c...  13 us
    ppermute x7, starting transfers between devices, overflow_round(): got.append(lax.ppermute(parts[m], AXES, pairs))  9.31 us
    all_to_all x1, starting transfers between devices, body(): first = lax.all_to_all(send, AXES, split_axis=0, concat_axis=0, tiled=True)  5.65 us
    pallas_call x1, Pallas kernels, split(): pl.pallas_call(functools.partial(split_kernel, per_step, wide, cols), gri...  5.62 us
    ppermute x2, waiting for transfers between devices, chip_sum(): got = lax.ppermute(give, 'col', [(c, c ^ 1) for c in range(cols)])  4.55 us
    unnamed x24, local copies, waits for them, and re-layouts  4.11 us
  transfers between devices with their start and end apart: 15, of which 10 were waited for; matrix products, arithmetic and copies ran while one was open for 1% of the time, Pallas kernels for 12%

profile of v2, /device:TPU:0, one launch (start us, length us, event | category | flops | bytes accessed | tf_op | source)
XLA Modules:
  0.0 112.9 jit_solution(14330873682804440207)
XLA Ops:
  0.0 3.8 %pack.2 = (f32[32,128,128]{2,1,0:T(8,128)}, f32[520,128]{1,0:T(8,128)S(1)}) custom-call(s32[1]{0:T(128)} %constant.67.clone.1.rnd, s32[32]{0:T(128)} %bitcast.80, s32[32]{0:T(128)} %occ.1, s32[32]{0:T(128)} %vir.1, f32[32,128,128]{2,1,0:T(8,128)} %amp.1), custom_call_target="tpu_custom_call" | custom-call | tf_op jit(solution)/shard_map/pack/pallas_call | solution.py:103
  3.8 4.0 %collective-permute-start.13 = (f32[520,128]{1,0:T(8,128)S(1)}, f32[520,128]{1,0:T(8,128)S(1)}, u32[]{:S(2)}, u32[]{:S(2)}) collective-permute-start(f32[520,128]{1,0:T(8,128)S(1)} %get-tuple-element.94.refs_0_), channel_id=1, source_target_pairs={{0,16},{1,17},{2,18},{3,19},{4,20},{5,21},{6,22},{7,23},{8,24},{9,... | collective-permute-start | bytes 798728 | tf_op jit(solution)/shard_map/ppermute | solution.py:171
  7.8 1.6 %collective-permute-start.12 = (f32[520,128]{1,0:T(8,128)S(1)}, f32[520,128]{1,0:T(8,128)S(1)}, u32[]{:S(2)}, u32[]{:S(2)}) collective-permute-start(f32[520,128]{1,0:T(8,128)S(1)} %get-tuple-element.94.refs_0_), channel_id=1, source_target_pairs={{0,8},{1,9},{2,10},{3,11},{4,12},{5,13},{6,14},{7,15},{8,0},{9,1},... | collective-permute-start | bytes 798728 | tf_op jit(solution)/shard_map/ppermute | solution.py:172
  9.5 3.4 %copy-done = f32[4096,4,128]{2,1,0:T(4,128)S(1)} copy-done((f32[4096,4,128]{2,1,0:T(4,128)S(1)}, f32[4096,4,128]{2,1,0:T(4,128)}, u32[]{:S(2)}) %copy-start) | copy-done | bytes 8388632
  12.9 5.6 %split.1.refs_9_ = bf16[32,256,512]{2,1,0:T(8,128)(2,1)} custom-call(s32[4]{0:T(128)S(1)} %pad_add_fusion.place, f32[16384,128]{1,0:T(8,128)S(1)} %bitcast.79), custom_call_target="tpu_custom_call" | custom-call | bytes 16777216 | tf_op jit(solution)/shard_map/split/pallas_call | solution.py:205
  18.5 1.5 %collective-permute-done.13.refs_2_ = f32[520,128]{1,0:T(8,128)S(1)} collective-permute-done((f32[520,128]{1,0:T(8,128)S(1)}, f32[520,128]{1,0:T(8,128)S(1)}, u32[]{:S(2)}, u32[]{:S(2)}) %collective-permute-start.13) | collective-permute-done | bytes 266272 | tf_op jit(solution)/shard_map/ppermute | solution.py:171
  20.6 5.7 %all-to-all-start = ((f32[32,128,128]{2,1,0:T(8,128)}), f32[32,128,128]{2,1,0:T(8,128)S(1)}, u32[]{:S(2)}, u32[]{:S(2)}) async-start(f32[32,128,128]{2,1,0:T(8,128)} %get-tuple-element.104), calls=%async_computation | async-start | bytes 4194304 | tf_op jit(solution)/shard_map/all_to_all | solution.py:381
  26.3 1.2 %collective-permute-done.14.refs_3_ = f32[520,128]{1,0:T(8,128)S(1)} collective-permute-done((f32[520,128]{1,0:T(8,128)S(1)}, f32[520,128]{1,0:T(8,128)S(1)}, u32[]{:S(2)}, u32[]{:S(2)}) %collective-permute-start.14) | collective-permute-done | bytes 266272 | tf_op jit(solution)/shard_map/ppermute | solution.py:174
  27.5 1.0 pick.2
  29.0 0.9 collective-permute-start.18
  29.9 1.6 %collective-permute-start.17 = (f32[544,128]{1,0:T(8,128)S(1)}, f32[544,128]{1,0:T(8,128)S(1)}, u32[]{:S(2)}, u32[]{:S(2)}) collective-permute-start(f32[544,128]{1,0:T(8,128)S(1)} %get-tuple-element.99), channel_id=1, source_target_pairs={{0,3},{1,2},{2,1},{3,0},{4,7},{5,6},{6,5},{7,4},{8,11},{9,10},{10,... | collective-permute-start | bytes 835592 | tf_op jit(solution)/shard_map/ppermute | solution.py:180
  32.1 17.1 %collective-permute-done.19.refs_5_ = f32[544,128]{1,0:T(8,128)S(1)} collective-permute-done((f32[544,128]{1,0:T(8,128)S(1)}, f32[544,128]{1,0:T(8,128)S(1)}, u32[]{:S(2)}, u32[]{:S(2)}) %collective-permute-start.19) | collective-permute-done | bytes 278560 | tf_op jit(solution)/shard_map/ppermute | solution.py:180
  49.2 4.5 %collective-permute-start.21 = (f32[544,128]{1,0:T(8,128)S(1)}, f32[544,128]{1,0:T(8,128)S(1)}, u32[]{:S(2)}, u32[]{:S(2)}) collective-permute-start(f32[544,128]{1,0:T(8,128)S(1)} %get-tuple-element.103), channel_id=1, source_target_pairs={{0,7},{1,6},{2,5},{3,4},{4,3},{5,2},{6,1},{7,0},{8,15},{9,14},{10,... | collective-permute-start | bytes 835592 | tf_op jit(solution)/shard_map/ppermute | solution.py:180
  53.7 6.3 %collective-permute-done.18.refs_4_ = f32[544,128]{1,0:T(8,128)S(1)} collective-permute-done((f32[544,128]{1,0:T(8,128)S(1)}, f32[544,128]{1,0:T(8,128)S(1)}, u32[]{:S(2)}, u32[]{:S(2)}) %collective-permute-start.18) | collective-permute-done | bytes 278560 | tf_op jit(solution)/shard_map/ppermute | solution.py:180
  60.0 1.3 %collective-permute-start.20 = (f32[544,128]{1,0:T(8,128)S(1)}, f32[544,128]{1,0:T(8,128)S(1)}, u32[]{:S(2)}, u32[]{:S(2)}) collective-permute-start(f32[544,128]{1,0:T(8,128)S(1)} %get-tuple-element.102), channel_id=1, source_target_pairs={{0,6},{1,7},{2,4},{3,5},{4,2},{5,3},{6,0},{7,1},{8,14},{9,15},{10,... | collective-permute-start | bytes 835592 | tf_op jit(solution)/shard_map/ppermute | solution.py:180
  61.4 6.6 %collective-permute-done.21.refs_7_ = f32[544,128]{1,0:T(8,128)S(1)} collective-permute-done((f32[544,128]{1,0:T(8,128)S(1)}, f32[544,128]{1,0:T(8,128)S(1)}, u32[]{:S(2)}, u32[]{:S(2)}) %collective-permute-start.21) | collective-permute-done | bytes 278560 | tf_op jit(solution)/shard_map/ppermute | solution.py:180
  68.0 9.1 %collective-permute-done.20.refs_6_ = f32[544,128]{1,0:T(8,128)S(1)} collective-permute-done((f32[544,128]{1,0:T(8,128)S(1)}, f32[544,128]{1,0:T(8,128)S(1)}, u32[]{:S(2)}, u32[]{:S(2)}) %collective-permute-start.20) | collective-permute-done | bytes 278560 | tf_op jit(solution)/shard_map/ppermute | solution.py:180
  78.3 6.4 %product.3 = (f32[2,1,640,128]{3,2,1,0:T(8,128)S(1)}, f32[2,1,640,128]{3,2,1,0:T(8,128)S(1)}) custom-call(s32[1]{0:T(128)} %constant.67.clone.1.rnd, s32[4]{0:T(128)S(1)} %pad_add_fusion.place, s32[32]{0:T(128)S(1)} %reshape.169.table, f32[544,128]{1,0:T(8,128)} %copy-done.2, f32[544,128]{1,0:T(8,128)} %copy-done.14, f32[544,128]{1,0:T(8,128)} %copy-done.13, ...), custom_call_target="tpu_custom_call" | custom-call | flops 1073741824 | bytes 16777216 | tf_op jit(solution)/shard_map/product/pallas_call | solution.py:333
  84.8 2.1 %collective-permute-done.22 = f32[2,1,640,128]{3,2,1,0:T(8,128)S(1)} collective-permute-done((f32[2,1,640,128]{3,2,1,0:T(8,128)S(1)}, f32[2,1,640,128]{3,2,1,0:T(8,128)S(1)}, u32[]{:S(2)}, u32[]{:S(2)}) %collective-permute-start.22) | collective-permute-done | bytes 655392 | tf_op jit(solution)/shard_map/ppermute | solution.py:355
  87.0 7.4 %product.4 = (f32[2,1,896,128]{3,2,1,0:T(8,128)S(1)}, f32[2,1,896,128]{3,2,1,0:T(8,128)S(1)}) custom-call(s32[1]{0:T(128)} %constant.67.clone.1.rnd, s32[4]{0:T(128)S(1)} %pad_add_fusion.place, s32[32]{0:T(128)S(1)} %reshape.169.table, f32[544,128]{1,0:T(8,128)} %copy-done.2, f32[544,128]{1,0:T(8,128)} %copy-done.14, f32[544,128]{1,0:T(8,128)} %copy-done.13, ...), custom_call_target="tpu_custom_call" | custom-call | flops 1073741824 | bytes 16777216 | tf_op jit(solution)/shard_map/product/pallas_call | solution.py:333
  94.4 2.3 %collective-permute-done.23 = f32[1,640,128]{2,1,0:T(8,128)S(1)} collective-permute-done((f32[1,640,128]{2,1,0:T(8,128)S(1)}, f32[1,640,128]{2,1,0:T(8,128)S(1)}, u32[]{:S(2)}, u32[]{:S(2)}) %collective-permute-start.23) | collective-permute-done | bytes 327712 | tf_op jit(solution)/shard_map/ppermute | solution.py:361
  96.7 2.5 %collective-permute-done.24 = f32[2,1,896,128]{3,2,1,0:T(8,128)S(1)} collective-permute-done((f32[2,1,896,128]{3,2,1,0:T(8,128)S(1)}, f32[2,1,896,128]{3,2,1,0:T(8,128)S(1)}, u32[]{:S(2)}, u32[]{:S(2)}) %collective-permute-start.24) | collective-permute-done | bytes 917536 | tf_op jit(solution)/shard_map/ppermute | solution.py:355
  101.2 10.7 %collective-permute-done.25 = f32[1,896,128]{2,1,0:T(8,128)S(1)} collective-permute-done((f32[1,896,128]{2,1,0:T(8,128)S(1)}, f32[1,896,128]{2,1,0:T(8,128)S(1)}, u32[]{:S(2)}, u32[]{:S(2)}) %collective-permute-start.25) | collective-permute-done | bytes 458784 | tf_op jit(solution)/shard_map/ppermute | solution.py:361
  112.0 0.9 pad_maximum_fusion
  (70 shorter events, 4.4 us)
Async XLA Ops:
  3.8 16.2 %collective-permute-start.13 = (f32[520,128]{1,0:T(8,128)S(1)}, f32[520,128]{1,0:T(8,128)S(1)}, u32[]{:S(2)}, u32[]{:S(2)}) collective-permute-start(f32[520,128]{1,0:T(8,128)S(1)} %get-tuple-element.94.refs_0_), channel_id=1, source_target_pairs={{0,16},{1,17},{2,18},{3,19},{4,20},{5,21},{6,22},{7,23},{8,24},{9,... | collective-permute-start | bytes 798728 | tf_op jit(solution)/shard_map/ppermute | solution.py:171
  7.8 18.5 %collective-permute-start.12 = (f32[520,128]{1,0:T(8,128)S(1)}, f32[520,128]{1,0:T(8,128)S(1)}, u32[]{:S(2)}, u32[]{:S(2)}) collective-permute-start(f32[520,128]{1,0:T(8,128)S(1)} %get-tuple-element.94.refs_0_), channel_id=1, source_target_pairs={{0,8},{1,9},{2,10},{3,11},{4,12},{5,13},{6,14},{7,15},{8,0},{9,1},... | collective-permute-start | bytes 798728 | tf_op jit(solution)/shard_map/ppermute | solution.py:172
  20.0 7.5 %collective-permute-start.14 = (f32[520,128]{1,0:T(8,128)S(1)}, f32[520,128]{1,0:T(8,128)S(1)}, u32[]{:S(2)}, u32[]{:S(2)}) collective-permute-start(f32[520,128]{1,0:T(8,128)S(1)} %collective-permute-done.13.refs_2_), channel_id=1, source_target_pairs={{0,8},{1,9},{2,10},{3,11},{4,12},{5,13},{6,14},{7,15},{8,0},{9,1},... | collective-permute-start | bytes 798728 | tf_op jit(solution)/shard_map/ppermute | solution.py:174
  20.6 57.6 %all-to-all-start = ((f32[32,128,128]{2,1,0:T(8,128)}), f32[32,128,128]{2,1,0:T(8,128)S(1)}, u32[]{:S(2)}, u32[]{:S(2)}) async-start(f32[32,128,128]{2,1,0:T(8,128)} %get-tuple-element.104), calls=%async_computation | async-start | bytes 4194304 | tf_op jit(solution)/shard_map/all_to_all | solution.py:381
  28.5 49.7 %copy-start.2 = (f32[544,128]{1,0:T(8,128)}, f32[544,128]{1,0:T(8,128)S(1)}, u32[]{:S(2)}) copy-start(f32[544,128]{1,0:T(8,128)S(1)} %get-tuple-element.96.refs_0_) | copy-start | bytes 835588
  28.6 20.6 %collective-permute-start.19 = (f32[544,128]{1,0:T(8,128)S(1)}, f32[544,128]{1,0:T(8,128)S(1)}, u32[]{:S(2)}, u32[]{:S(2)}) collective-permute-start(f32[544,128]{1,0:T(8,128)S(1)} %get-tuple-element.101), channel_id=1, source_target_pairs={{0,5},{1,4},{2,7},{3,6},{4,1},{5,0},{6,3},{7,2},{8,13},{9,12},{10,... | collective-permute-start | bytes 835592 | tf_op jit(solution)/shard_map/ppermute | solution.py:180
  29.0 31.0 %collective-permute-start.18 = (f32[544,128]{1,0:T(8,128)S(1)}, f32[544,128]{1,0:T(8,128)S(1)}, u32[]{:S(2)}, u32[]{:S(2)}) collective-permute-start(f32[544,128]{1,0:T(8,128)S(1)} %get-tuple-element.100), channel_id=1, source_target_pairs={{0,4},{1,5},{2,6},{3,7},{4,0},{5,1},{6,2},{7,3},{8,12},{9,13},{10,... | collective-permute-start | bytes 835592 | tf_op jit(solution)/shard_map/ppermute | solution.py:180
  29.9 31.4 %collective-permute-start.17 = (f32[544,128]{1,0:T(8,128)S(1)}, f32[544,128]{1,0:T(8,128)S(1)}, u32[]{:S(2)}, u32[]{:S(2)}) collective-permute-start(f32[544,128]{1,0:T(8,128)S(1)} %get-tuple-element.99), channel_id=1, source_target_pairs={{0,3},{1,2},{2,1},{3,0},{4,7},{5,6},{6,5},{7,4},{8,11},{9,10},{10,... | collective-permute-start | bytes 835592 | tf_op jit(solution)/shard_map/ppermute | solution.py:180
  31.5 29.8 %collective-permute-start.16 = (f32[544,128]{1,0:T(8,128)S(1)}, f32[544,128]{1,0:T(8,128)S(1)}, u32[]{:S(2)}, u32[]{:S(2)}) collective-permute-start(f32[544,128]{1,0:T(8,128)S(1)} %get-tuple-element.98), channel_id=1, source_target_pairs={{0,2},{1,3},{2,0},{3,1},{4,6},{5,7},{6,4},{7,5},{8,10},{9,11},{10,... | collective-permute-start | bytes 835592 | tf_op jit(solution)/shard_map/ppermute | solution.py:180
  32.1 29.3 %collective-permute-start.15 = (f32[544,128]{1,0:T(8,128)S(1)}, f32[544,128]{1,0:T(8,128)S(1)}, u32[]{:S(2)}, u32[]{:S(2)}) collective-permute-start(f32[544,128]{1,0:T(8,128)S(1)} %get-tuple-element.97), channel_id=1, source_target_pairs={{0,1},{1,0},{2,3},{3,2},{4,5},{5,4},{6,7},{7,6},{8,9},{9,8},{10,11... | collective-permute-start | bytes 835592 | tf_op jit(solution)/shard_map/ppermute | solution.py:180
  49.2 29.0 %copy-start.10 = (f32[544,128]{1,0:T(8,128)}, f32[544,128]{1,0:T(8,128)S(1)}, u32[]{:S(2)}) copy-start(f32[544,128]{1,0:T(8,128)S(1)} %collective-permute-done.19.refs_5_) | copy-start | bytes 835588
  49.2 18.8 %collective-permute-start.21 = (f32[544,128]{1,0:T(8,128)S(1)}, f32[544,128]{1,0:T(8,128)S(1)}, u32[]{:S(2)}, u32[]{:S(2)}) collective-permute-start(f32[544,128]{1,0:T(8,128)S(1)} %get-tuple-element.103), channel_id=1, source_target_pairs={{0,7},{1,6},{2,5},{3,4},{4,3},{5,2},{6,1},{7,0},{8,15},{9,14},{10,... | collective-permute-start | bytes 835592 | tf_op jit(solution)/shard_map/ppermute | solution.py:180
  60.0 18.2 %copy-start.11 = (f32[544,128]{1,0:T(8,128)}, f32[544,128]{1,0:T(8,128)S(1)}, u32[]{:S(2)}) copy-start(f32[544,128]{1,0:T(8,128)S(1)} %collective-permute-done.18.refs_4_) | copy-start | bytes 835588
  60.0 17.1 %collective-permute-start.20 = (f32[544,128]{1,0:T(8,128)S(1)}, f32[544,128]{1,0:T(8,128)S(1)}, u32[]{:S(2)}, u32[]{:S(2)}) collective-permute-start(f32[544,128]{1,0:T(8,128)S(1)} %get-tuple-element.102), channel_id=1, source_target_pairs={{0,6},{1,7},{2,4},{3,5},{4,2},{5,3},{6,0},{7,1},{8,14},{9,15},{10,... | collective-permute-start | bytes 835592 | tf_op jit(solution)/shard_map/ppermute | solution.py:180
  61.3 16.9 %copy-start.12 = (f32[544,128]{1,0:T(8,128)}, f32[544,128]{1,0:T(8,128)S(1)}, u32[]{:S(2)}) copy-start(f32[544,128]{1,0:T(8,128)S(1)} %collective-permute-done.17.refs_3_) | copy-start | bytes 835588
  61.3 15.8 %copy-start.13 = (f32[544,128]{1,0:T(8,128)}, f32[544,128]{1,0:T(8,128)S(1)}, u32[]{:S(2)}) copy-start(f32[544,128]{1,0:T(8,128)S(1)} %collective-permute-done.16.refs_2_) | copy-start | bytes 835588
  61.4 15.8 %copy-start.14 = (f32[544,128]{1,0:T(8,128)}, f32[544,128]{1,0:T(8,128)S(1)}, u32[]{:S(2)}) copy-start(f32[544,128]{1,0:T(8,128)S(1)} %collective-permute-done.15.refs_1_) | copy-start | bytes 835588
  84.7 2.2 %collective-permute-start.22 = (f32[2,1,640,128]{3,2,1,0:T(8,128)S(1)}, f32[2,1,640,128]{3,2,1,0:T(8,128)S(1)}, u32[]{:S(2)}, u32[]{:S(2)}) collective-permute-start(f32[2,1,640,128]{3,2,1,0:T(8,128)S(1)} %get-tuple-element.107), channel_id=1, source_target_pairs={{0,1},{1,0},{2,3},{3,2},{4,5},{5,4},{6,7},{7,6},{8,9},{9,8},{10,11... | collective-permute-start | bytes 1966088 | tf_op jit(solution)/shard_map/ppermute | solution.py:355
  86.9 9.8 %collective-permute-start.23 = (f32[1,640,128]{2,1,0:T(8,128)S(1)}, f32[1,640,128]{2,1,0:T(8,128)S(1)}, u32[]{:S(2)}, u32[]{:S(2)}) collective-permute-start(f32[1,640,128]{2,1,0:T(8,128)S(1)} %get-tuple-element.111), channel_id=1, source_target_pairs={{0,2},{1,3},{2,0},{3,1},{4,6},{5,7},{6,4},{7,5},{8,10},{9,11},{10,... | collective-permute-start | bytes 983048 | tf_op jit(solution)/shard_map/ppermute | solution.py:361
  96.7 2.5 %collective-permute-start.24 = (f32[2,1,896,128]{3,2,1,0:T(8,128)S(1)}, f32[2,1,896,128]{3,2,1,0:T(8,128)S(1)}, u32[]{:S(2)}, u32[]{:S(2)}) collective-permute-start(f32[2,1,896,128]{3,2,1,0:T(8,128)S(1)} %get-tuple-element.114), channel_id=1, source_target_pairs={{0,1},{1,0},{2,3},{3,2},{4,5},{5,4},{6,7},{7,6},{8,9},{9,8},{10,11... | collective-permute-start | bytes 2752520 | tf_op jit(solution)/shard_map/ppermute | solution.py:355
  99.3 12.6 %collective-permute-start.25 = (f32[1,896,128]{2,1,0:T(8,128)S(1)}, f32[1,896,128]{2,1,0:T(8,128)S(1)}, u32[]{:S(2)}, u32[]{:S(2)}) collective-permute-start(f32[1,896,128]{2,1,0:T(8,128)S(1)} %get-tuple-element.116), channel_id=1, source_target_pairs={{0,2},{1,3},{2,0},{3,1},{4,6},{5,7},{6,4},{7,5},{8,10},{9,11},{10,... | collective-permute-start | bytes 1376264 | tf_op jit(solution)/shard_map/ppermute | solution.py:361
  101.2 11.8 %copy-start.17 = (s32[32,1]{0,1:T(1,128)S(1)}, s32[32,1]{0,1:T(1,128)}, u32[]{:S(2)}) copy-start(s32[32,1]{0,1:T(1,128)} %param.8) | copy-start | bytes 388
  101.2 11.7 %copy-start.18 = (s32[32]{0:T(128)S(1)}, s32[32]{0:T(128)}, u32[]{:S(2)}) copy-start(s32[32]{0:T(128)} %occ.1) | copy-start | bytes 388
  101.2 11.7 %copy-start.19 = (s32[32]{0:T(128)S(1)}, s32[32]{0:T(128)}, u32[]{:S(2)}) copy-start(s32[32]{0:T(128)} %vir.1) | copy-start | bytes 388
  (3 other events, 13.3 us)

commit v3 on v2

--- a/solution.py
+++ b/solution.py
@@ -218,7 +218,7 @@
 
 
 def product_kernel(layer, firsts, low_occ, occs, per_round, cols, own, rnd, place, table, *refs):
-    sources, refs = refs[:layer], refs[layer:]
+    sources, refs = refs[:layer][::-1], refs[layer:]
     if firsts:
         first, refs = refs[0], refs[1:]
     both, keep, give, tiles, held, queue, sem_t, sem_b = refs
@@ -277,7 +277,7 @@
     if firsts:
 
         def listing(i, n):
-            m, at = i // NZ, i % NZ
+            m, at = layer - 1 - i // NZ, i % NZ
             return enter(0, n, at * layer + (mine ^ m), table[i] & MASK, True)[1]
 
         total = lax.fori_loop(0, count, listing, total, unroll=4)
@@ -289,7 +289,7 @@
     seconds = jnp.int32(0)
     for m in range(layer):
         for k in range(NZ):
-            code = table[m * NZ + k]
+            code = table[(layer - 1 - m) * NZ + k]
             here = (code >> (2 * SHIFT)) - rnd[0] * per_round
             ok, more = enter(GROUP * early, seconds, seconds, (code >> SHIFT) & MASK, (here >= 0) & (here < per_round))
 
@@ -326,7 +326,7 @@
     chips = cols // 2
     count = layer * NZ
     firsts = first is not None
-    operands = [pltpu.with_memory_space_constraint(a, pltpu.HBM) for a in second]
+    operands = [pltpu.with_memory_space_constraint(a, pltpu.HBM) for a in reversed(second)]
     if firsts:
         operands.append(pltpu.with_memory_space_constraint(first, pltpu.VMEM))
     out = pltpu.VMEM((chips, own, rows, edge), f32)
@@ -380,7 +380,7 @@
     send, pay = packed(zero)
     first = lax.all_to_all(send, AXES, split_axis=0, concat_axis=0, tiled=True)
     got, both = overflow_round(zero, place, pay, layer, per_round, split(place, integrals, cols))
-    heads = jnp.stack([g[NZ * edge :].reshape(NZ, HEAD, 128)[:, 0] for g in got]).astype(jnp.int32)
+    heads = jnp.stack([g[NZ * edge :].reshape(NZ, HEAD, 128)[:, 0] for g in reversed(got)]).astype(jnp.int32)
     table = lax.dynamic_index_in_dim(heads, me, 2, keepdims=False).reshape(-1)
     most = jnp.max(jnp.sum(((heads >> SHIFT) & MASK) > 0, axis=2, dtype=jnp.int32))
     rounds = (most + per_round - 1) // per_round

time: 112 us -> 113 us (level)
  Pallas kernels: 24.3 us -> 19.6 us
  waiting for transfers between devices: 59.4 us -> 63.3 us
    pallas_call x2, Pallas kernels: 13.8 us -> 9.21 us  [product(): pl.pallas_call(functools.partial(product_kernel, layer, firsts, low_occ,...]
    ppermute x2, starting transfers between devices: 0.07 us -> 3.17 us  [chip_sum(): got = lax.ppermute(give, 'col', [(c, c ^ 1) for c in range(cols)])]
    ppermute x2, waiting for transfers between devices: 13 us -> 15.5 us  [exchange(): lax.ppermute(sums[j], 'col', [(c, (c // 2 + j) % chips * 2 + c % 2) for c...]
    ppermute x7, starting transfers between devices: 9.31 us -> 7.26 us  [overflow_round(): got.append(lax.ppermute(parts[m], AXES, pairs))]
    ppermute x7, waiting for transfers between devices: 39.2 us -> 40.5 us  [overflow_round(): got.append(lax.ppermute(parts[m], AXES, pairs))]
  transfers between devices with their start and end apart: 15 -> 15, of which waited for: 10 -> 10; matrix products, arithmetic and copies ran while one was open for 1% -> 1% of each run, Pallas kernels for 12% -> 10%
where the time goes in v3:
time: 113 us
  waiting for transfers between devices  63.3 us (56%)
  starting transfers between devices  22.6 us (20%)
  Pallas kernels  19.6 us (17%)
  local copies, waits for them, and re-layouts  4.54 us (4%)
  other arithmetic  2.06 us (2%)
    ppermute x7, waiting for transfers between devices, overflow_round(): got.append(lax.ppermute(parts[m], AXES, pairs))  40.5 us
    ppermute x2, waiting for transfers between devices, exchange(): lax.ppermute(sums[j], 'col', [(c, (c // 2 + j) % chips * 2 + c % 2) for c...  15.5 us
    pallas_call x2, Pallas kernels, product(): pl.pallas_call(functools.partial(product_kernel, layer, firsts, low_occ,...  9.21 us
    ppermute x7, starting transfers between devices, overflow_round(): got.append(lax.ppermute(parts[m], AXES, pairs))  7.26 us
    pallas_call x1, Pallas kernels, split(): pl.pallas_call(functools.partial(split_kernel, per_step, wide, cols), gri...  5.62 us
    all_to_all x1, starting transfers between devices, body(): first = lax.all_to_all(send, AXES, split_axis=0, concat_axis=0, tiled=True)  5.53 us
    ppermute x2, waiting for transfers between devices, chip_sum(): got = lax.ppermute(give, 'col', [(c, c ^ 1) for c in range(cols)])  4.19 us
    unnamed x24, local copies, waits for them, and re-layouts  4.16 us
  transfers between devices with their start and end apart: 15, of which 10 were waited for; matrix products, arithmetic and copies ran while one was open for 1% of the time, Pallas kernels for 10%

profile of v3, /device:TPU:0, one launch (start us, length us, event | category | flops | bytes accessed | tf_op | source)
XLA Modules:
  0.0 113.1 jit_solution(14158783564523110229)
XLA Ops:
  0.0 3.7 %pack.2 = (f32[32,128,128]{2,1,0:T(8,128)}, f32[520,128]{1,0:T(8,128)S(1)}) custom-call(s32[1]{0:T(128)} %constant.67.clone.1.rnd, s32[32]{0:T(128)} %bitcast.80, s32[32]{0:T(128)} %occ.1, s32[32]{0:T(128)} %vir.1, f32[32,128,128]{2,1,0:T(8,128)} %amp.1), custom_call_target="tpu_custom_call" | custom-call | tf_op jit(solution)/shard_map/pack/pallas_call | solution.py:103
  3.7 4.1 %collective-permute-start.13 = (f32[520,128]{1,0:T(8,128)S(1)}, f32[520,128]{1,0:T(8,128)S(1)}, u32[]{:S(2)}, u32[]{:S(2)}) collective-permute-start(f32[520,128]{1,0:T(8,128)S(1)} %get-tuple-element.94.refs_0_), channel_id=1, source_target_pairs={{0,16},{1,17},{2,18},{3,19},{4,20},{5,21},{6,22},{7,23},{8,24},{9,... | collective-permute-start | bytes 798728 | tf_op jit(solution)/shard_map/ppermute | solution.py:171
  7.8 1.6 %collective-permute-start.12 = (f32[520,128]{1,0:T(8,128)S(1)}, f32[520,128]{1,0:T(8,128)S(1)}, u32[]{:S(2)}, u32[]{:S(2)}) collective-permute-start(f32[520,128]{1,0:T(8,128)S(1)} %get-tuple-element.94.refs_0_), channel_id=1, source_target_pairs={{0,8},{1,9},{2,10},{3,11},{4,12},{5,13},{6,14},{7,15},{8,0},{9,1},... | collective-permute-start | bytes 798728 | tf_op jit(solution)/shard_map/ppermute | solution.py:172
  9.4 3.4 %copy-done = f32[4096,4,128]{2,1,0:T(4,128)S(1)} copy-done((f32[4096,4,128]{2,1,0:T(4,128)S(1)}, f32[4096,4,128]{2,1,0:T(4,128)}, u32[]{:S(2)}) %copy-start) | copy-done | bytes 8388632
  12.8 5.6 %split.1.refs_9_ = bf16[32,256,512]{2,1,0:T(8,128)(2,1)} custom-call(s32[4]{0:T(128)S(1)} %pad_add_fusion.place, f32[16384,128]{1,0:T(8,128)S(1)} %bitcast.79), custom_call_target="tpu_custom_call" | custom-call | bytes 16777216 | tf_op jit(solution)/shard_map/split/pallas_call | solution.py:205
  18.4 1.6 %collective-permute-done.13.refs_2_ = f32[520,128]{1,0:T(8,128)S(1)} collective-permute-done((f32[520,128]{1,0:T(8,128)S(1)}, f32[520,128]{1,0:T(8,128)S(1)}, u32[]{:S(2)}, u32[]{:S(2)}) %collective-permute-start.13) | collective-permute-done | bytes 266272 | tf_op jit(solution)/shard_map/ppermute | solution.py:171
  20.7 5.5 %all-to-all-start = ((f32[32,128,128]{2,1,0:T(8,128)}), f32[32,128,128]{2,1,0:T(8,128)S(1)}, u32[]{:S(2)}, u32[]{:S(2)}) async-start(f32[32,128,128]{2,1,0:T(8,128)} %get-tuple-element.104), calls=%async_computation | async-start | bytes 4194304 | tf_op jit(solution)/shard_map/all_to_all | solution.py:381
  26.3 1.4 %collective-permute-done.14.refs_3_ = f32[520,128]{1,0:T(8,128)S(1)} collective-permute-done((f32[520,128]{1,0:T(8,128)S(1)}, f32[520,128]{1,0:T(8,128)S(1)}, u32[]{:S(2)}, u32[]{:S(2)}) %collective-permute-start.14) | collective-permute-done | bytes 266272 | tf_op jit(solution)/shard_map/ppermute | solution.py:174
  27.7 1.1 pick.2
  28.8 1.3 %collective-permute-start.20 = (f32[544,128]{1,0:T(8,128)S(1)}, f32[544,128]{1,0:T(8,128)S(1)}, u32[]{:S(2)}, u32[]{:S(2)}) collective-permute-start(f32[544,128]{1,0:T(8,128)S(1)} %get-tuple-element.101), channel_id=1, source_target_pairs={{0,2},{1,3},{2,0},{3,1},{4,6},{5,7},{6,4},{7,5},{8,10},{9,11},{10,... | collective-permute-start | bytes 835592 | tf_op jit(solution)/shard_map/ppermute | solution.py:180
  30.1 1.5 %collective-permute-start.18 = (f32[544,128]{1,0:T(8,128)S(1)}, f32[544,128]{1,0:T(8,128)S(1)}, u32[]{:S(2)}, u32[]{:S(2)}) collective-permute-start(f32[544,128]{1,0:T(8,128)S(1)} %get-tuple-element.99), channel_id=1, source_target_pairs={{0,4},{1,5},{2,6},{3,7},{4,0},{5,1},{6,2},{7,3},{8,12},{9,13},{10,... | collective-permute-start | bytes 835592 | tf_op jit(solution)/shard_map/ppermute | solution.py:180
  32.4 2.2 %collective-permute-start.16 = (f32[544,128]{1,0:T(8,128)S(1)}, f32[544,128]{1,0:T(8,128)S(1)}, u32[]{:S(2)}, u32[]{:S(2)}) collective-permute-start(f32[544,128]{1,0:T(8,128)S(1)} %get-tuple-element.97), channel_id=1, source_target_pairs={{0,6},{1,7},{2,4},{3,5},{4,2},{5,3},{6,0},{7,1},{8,14},{9,15},{10,... | collective-permute-start | bytes 835592 | tf_op jit(solution)/shard_map/ppermute | solution.py:180
  34.5 19.1 %collective-permute-done.20.refs_5_ = f32[544,128]{1,0:T(8,128)S(1)} collective-permute-done((f32[544,128]{1,0:T(8,128)S(1)}, f32[544,128]{1,0:T(8,128)S(1)}, u32[]{:S(2)}, u32[]{:S(2)}) %collective-permute-start.20) | collective-permute-done | bytes 278560 | tf_op jit(solution)/shard_map/ppermute | solution.py:180
  54.0 6.2 %collective-permute-done.19.refs_4_ = f32[544,128]{1,0:T(8,128)S(1)} collective-permute-done((f32[544,128]{1,0:T(8,128)S(1)}, f32[544,128]{1,0:T(8,128)S(1)}, u32[]{:S(2)}, u32[]{:S(2)}) %collective-permute-start.19) | collective-permute-done | bytes 278560 | tf_op jit(solution)/shard_map/ppermute | solution.py:180
  60.2 1.1 %collective-permute-start.21 = (f32[544,128]{1,0:T(8,128)S(1)}, f32[544,128]{1,0:T(8,128)S(1)}, u32[]{:S(2)}, u32[]{:S(2)}) collective-permute-start(f32[544,128]{1,0:T(8,128)S(1)} %get-tuple-element.102), channel_id=1, source_target_pairs={{0,1},{1,0},{2,3},{3,2},{4,5},{5,4},{6,7},{7,6},{8,9},{9,8},{10,11... | collective-permute-start | bytes 835592 | tf_op jit(solution)/shard_map/ppermute | solution.py:180
  61.4 9.4 %collective-permute-done.16.refs_1_ = f32[544,128]{1,0:T(8,128)S(1)} collective-permute-done((f32[544,128]{1,0:T(8,128)S(1)}, f32[544,128]{1,0:T(8,128)S(1)}, u32[]{:S(2)}, u32[]{:S(2)}) %collective-permute-start.16) | collective-permute-done | bytes 278560 | tf_op jit(solution)/shard_map/ppermute | solution.py:180
  70.8 5.8 %collective-permute-done.15.refs_0_ = f32[544,128]{1,0:T(8,128)S(1)} collective-permute-done((f32[544,128]{1,0:T(8,128)S(1)}, f32[544,128]{1,0:T(8,128)S(1)}, u32[]{:S(2)}, u32[]{:S(2)}) %collective-permute-start.15) | collective-permute-done | bytes 278560 | tf_op jit(solution)/shard_map/ppermute | solution.py:180
  77.8 4.0 %product.3 = (f32[2,1,640,128]{3,2,1,0:T(8,128)S(1)}, f32[2,1,640,128]{3,2,1,0:T(8,128)S(1)}) custom-call(s32[1]{0:T(128)} %constant.67.clone.1.rnd, s32[4]{0:T(128)S(1)} %pad_add_fusion.place, s32[32]{0:T(128)S(1)} %reshape.169.table, f32[544,128]{1,0:T(8,128)} %copy-done.15, f32[544,128]{1,0:T(8,128)} %copy-done.14, f32[544,128]{1,0:T(8,128)} %copy-done.13, ...), custom_call_target="tpu_custom_call" | custom-call | flops 1073741824 | bytes 16777216 | tf_op jit(solution)/shard_map/product/pallas_call | solution.py:333
  81.9 3.2 %collective-permute-start.22 = (f32[2,1,640,128]{3,2,1,0:T(8,128)S(1)}, f32[2,1,640,128]{3,2,1,0:T(8,128)S(1)}, u32[]{:S(2)}, u32[]{:S(2)}) collective-permute-start(f32[2,1,640,128]{3,2,1,0:T(8,128)S(1)} %get-tuple-element.107), channel_id=1, source_target_pairs={{0,1},{1,0},{2,3},{3,2},{4,5},{5,4},{6,7},{7,6},{8,9},{9,8},{10,11... | collective-permute-start | bytes 1966088 | tf_op jit(solution)/shard_map/ppermute | solution.py:355
  85.0 1.7 %collective-permute-done.22 = f32[2,1,640,128]{3,2,1,0:T(8,128)S(1)} collective-permute-done((f32[2,1,640,128]{3,2,1,0:T(8,128)S(1)}, f32[2,1,640,128]{3,2,1,0:T(8,128)S(1)}, u32[]{:S(2)}, u32[]{:S(2)}) %collective-permute-start.22) | collective-permute-done | bytes 655392 | tf_op jit(solution)/shard_map/ppermute | solution.py:355
  86.9 5.2 %product.4 = (f32[2,1,896,128]{3,2,1,0:T(8,128)S(1)}, f32[2,1,896,128]{3,2,1,0:T(8,128)S(1)}) custom-call(s32[1]{0:T(128)} %constant.67.clone.1.rnd, s32[4]{0:T(128)S(1)} %pad_add_fusion.place, s32[32]{0:T(128)S(1)} %reshape.169.table, f32[544,128]{1,0:T(8,128)} %copy-done.15, f32[544,128]{1,0:T(8,128)} %copy-done.14, f32[544,128]{1,0:T(8,128)} %copy-done.13, ...), custom_call_target="tpu_custom_call" | custom-call | flops 1073741824 | bytes 16777216 | tf_op jit(solution)/shard_map/product/pallas_call | solution.py:333
  92.1 4.8 %collective-permute-done.23 = f32[1,640,128]{2,1,0:T(8,128)S(1)} collective-permute-done((f32[1,640,128]{2,1,0:T(8,128)S(1)}, f32[1,640,128]{2,1,0:T(8,128)S(1)}, u32[]{:S(2)}, u32[]{:S(2)}) %collective-permute-start.23) | collective-permute-done | bytes 327712 | tf_op jit(solution)/shard_map/ppermute | solution.py:361
  96.9 2.5 %collective-permute-done.24 = f32[2,1,896,128]{3,2,1,0:T(8,128)S(1)} collective-permute-done((f32[2,1,896,128]{3,2,1,0:T(8,128)S(1)}, f32[2,1,896,128]{3,2,1,0:T(8,128)S(1)}, u32[]{:S(2)}, u32[]{:S(2)}) %collective-permute-start.24) | collective-permute-done | bytes 917536 | tf_op jit(solution)/shard_map/ppermute | solution.py:355
  101.3 10.7 %collective-permute-done.25 = f32[1,896,128]{2,1,0:T(8,128)S(1)} collective-permute-done((f32[1,896,128]{2,1,0:T(8,128)S(1)}, f32[1,896,128]{2,1,0:T(8,128)S(1)}, u32[]{:S(2)}, u32[]{:S(2)}) %collective-permute-start.25) | collective-permute-done | bytes 458784 | tf_op jit(solution)/shard_map/ppermute | solution.py:361
  (70 shorter events, 5.4 us)
Async XLA Ops:
  3.7 16.4 %collective-permute-start.13 = (f32[520,128]{1,0:T(8,128)S(1)}, f32[520,128]{1,0:T(8,128)S(1)}, u32[]{:S(2)}, u32[]{:S(2)}) collective-permute-start(f32[520,128]{1,0:T(8,128)S(1)} %get-tuple-element.94.refs_0_), channel_id=1, source_target_pairs={{0,16},{1,17},{2,18},{3,19},{4,20},{5,21},{6,22},{7,23},{8,24},{9,... | collective-permute-start | bytes 798728 | tf_op jit(solution)/shard_map/ppermute | solution.py:171
  7.8 18.5 %collective-permute-start.12 = (f32[520,128]{1,0:T(8,128)S(1)}, f32[520,128]{1,0:T(8,128)S(1)}, u32[]{:S(2)}, u32[]{:S(2)}) collective-permute-start(f32[520,128]{1,0:T(8,128)S(1)} %get-tuple-element.94.refs_0_), channel_id=1, source_target_pairs={{0,8},{1,9},{2,10},{3,11},{4,12},{5,13},{6,14},{7,15},{8,0},{9,1},... | collective-permute-start | bytes 798728 | tf_op jit(solution)/shard_map/ppermute | solution.py:172
  20.1 7.6 %collective-permute-start.14 = (f32[520,128]{1,0:T(8,128)S(1)}, f32[520,128]{1,0:T(8,128)S(1)}, u32[]{:S(2)}, u32[]{:S(2)}) collective-permute-start(f32[520,128]{1,0:T(8,128)S(1)} %collective-permute-done.13.refs_2_), channel_id=1, source_target_pairs={{0,8},{1,9},{2,10},{3,11},{4,12},{5,13},{6,14},{7,15},{8,0},{9,1},... | collective-permute-start | bytes 798728 | tf_op jit(solution)/shard_map/ppermute | solution.py:174
  20.7 57.1 %all-to-all-start = ((f32[32,128,128]{2,1,0:T(8,128)}), f32[32,128,128]{2,1,0:T(8,128)S(1)}, u32[]{:S(2)}, u32[]{:S(2)}) async-start(f32[32,128,128]{2,1,0:T(8,128)} %get-tuple-element.104), calls=%async_computation | async-start | bytes 4194304 | tf_op jit(solution)/shard_map/all_to_all | solution.py:381
  28.8 49.0 %copy-start.2 = (f32[544,128]{1,0:T(8,128)}, f32[544,128]{1,0:T(8,128)S(1)}, u32[]{:S(2)}) copy-start(f32[544,128]{1,0:T(8,128)S(1)} %get-tuple-element.103.refs_7_) | copy-start | bytes 835588
  28.8 24.8 %collective-permute-start.20 = (f32[544,128]{1,0:T(8,128)S(1)}, f32[544,128]{1,0:T(8,128)S(1)}, u32[]{:S(2)}, u32[]{:S(2)}) collective-permute-start(f32[544,128]{1,0:T(8,128)S(1)} %get-tuple-element.101), channel_id=1, source_target_pairs={{0,2},{1,3},{2,0},{3,1},{4,6},{5,7},{6,4},{7,5},{8,10},{9,11},{10,... | collective-permute-start | bytes 835592 | tf_op jit(solution)/shard_map/ppermute | solution.py:180
  30.1 30.2 %collective-permute-start.19 = (f32[544,128]{1,0:T(8,128)S(1)}, f32[544,128]{1,0:T(8,128)S(1)}, u32[]{:S(2)}, u32[]{:S(2)}) collective-permute-start(f32[544,128]{1,0:T(8,128)S(1)} %get-tuple-element.100), channel_id=1, source_target_pairs={{0,3},{1,2},{2,1},{3,0},{4,7},{5,6},{6,5},{7,4},{8,11},{9,10},{10,... | collective-permute-start | bytes 835592 | tf_op jit(solution)/shard_map/ppermute | solution.py:180
  30.1 31.3 %collective-permute-start.18 = (f32[544,128]{1,0:T(8,128)S(1)}, f32[544,128]{1,0:T(8,128)S(1)}, u32[]{:S(2)}, u32[]{:S(2)}) collective-permute-start(f32[544,128]{1,0:T(8,128)S(1)} %get-tuple-element.99), channel_id=1, source_target_pairs={{0,4},{1,5},{2,6},{3,7},{4,0},{5,1},{6,2},{7,3},{8,12},{9,13},{10,... | collective-permute-start | bytes 835592 | tf_op jit(solution)/shard_map/ppermute | solution.py:180
  31.6 29.8 %collective-permute-start.17 = (f32[544,128]{1,0:T(8,128)S(1)}, f32[544,128]{1,0:T(8,128)S(1)}, u32[]{:S(2)}, u32[]{:S(2)}) collective-permute-start(f32[544,128]{1,0:T(8,128)S(1)} %get-tuple-element.98), channel_id=1, source_target_pairs={{0,5},{1,4},{2,7},{3,6},{4,1},{5,0},{6,3},{7,2},{8,13},{9,12},{10,... | collective-permute-start | bytes 835592 | tf_op jit(solution)/shard_map/ppermute | solution.py:180
  32.4 38.5 %collective-permute-start.16 = (f32[544,128]{1,0:T(8,128)S(1)}, f32[544,128]{1,0:T(8,128)S(1)}, u32[]{:S(2)}, u32[]{:S(2)}) collective-permute-start(f32[544,128]{1,0:T(8,128)S(1)} %get-tuple-element.97), channel_id=1, source_target_pairs={{0,6},{1,7},{2,4},{3,5},{4,2},{5,3},{6,0},{7,1},{8,14},{9,15},{10,... | collective-permute-start | bytes 835592 | tf_op jit(solution)/shard_map/ppermute | solution.py:180
  53.6 24.2 %copy-start.10 = (f32[544,128]{1,0:T(8,128)}, f32[544,128]{1,0:T(8,128)S(1)}, u32[]{:S(2)}) copy-start(f32[544,128]{1,0:T(8,128)S(1)} %collective-permute-done.20.refs_5_) | copy-start | bytes 835588
  53.6 23.0 %collective-permute-start.15 = (f32[544,128]{1,0:T(8,128)S(1)}, f32[544,128]{1,0:T(8,128)S(1)}, u32[]{:S(2)}, u32[]{:S(2)}) collective-permute-start(f32[544,128]{1,0:T(8,128)S(1)} %get-tuple-element.96), channel_id=1, source_target_pairs={{0,7},{1,6},{2,5},{3,4},{4,3},{5,2},{6,1},{7,0},{8,15},{9,14},{10,... | collective-permute-start | bytes 835592 | tf_op jit(solution)/shard_map/ppermute | solution.py:180
  60.2 17.6 %copy-start.11 = (f32[544,128]{1,0:T(8,128)}, f32[544,128]{1,0:T(8,128)S(1)}, u32[]{:S(2)}) copy-start(f32[544,128]{1,0:T(8,128)S(1)} %collective-permute-done.19.refs_4_) | copy-start | bytes 835588
  60.2 16.4 %collective-permute-start.21 = (f32[544,128]{1,0:T(8,128)S(1)}, f32[544,128]{1,0:T(8,128)S(1)}, u32[]{:S(2)}, u32[]{:S(2)}) collective-permute-start(f32[544,128]{1,0:T(8,128)S(1)} %get-tuple-element.102), channel_id=1, source_target_pairs={{0,1},{1,0},{2,3},{3,2},{4,5},{5,4},{6,7},{7,6},{8,9},{9,8},{10,11... | collective-permute-start | bytes 835592 | tf_op jit(solution)/shard_map/ppermute | solution.py:180
  61.4 16.4 %copy-start.12 = (f32[544,128]{1,0:T(8,128)}, f32[544,128]{1,0:T(8,128)S(1)}, u32[]{:S(2)}) copy-start(f32[544,128]{1,0:T(8,128)S(1)} %collective-permute-done.18.refs_3_) | copy-start | bytes 835588
  61.4 15.3 %copy-start.13 = (f32[544,128]{1,0:T(8,128)}, f32[544,128]{1,0:T(8,128)S(1)}, u32[]{:S(2)}) copy-start(f32[544,128]{1,0:T(8,128)S(1)} %collective-permute-done.17.refs_2_) | copy-start | bytes 835588
  70.8 5.9 %copy-start.14 = (f32[544,128]{1,0:T(8,128)}, f32[544,128]{1,0:T(8,128)S(1)}, u32[]{:S(2)}) copy-start(f32[544,128]{1,0:T(8,128)S(1)} %collective-permute-done.16.refs_1_) | copy-start | bytes 835588
  81.9 4.9 %collective-permute-start.22 = (f32[2,1,640,128]{3,2,1,0:T(8,128)S(1)}, f32[2,1,640,128]{3,2,1,0:T(8,128)S(1)}, u32[]{:S(2)}, u32[]{:S(2)}) collective-permute-start(f32[2,1,640,128]{3,2,1,0:T(8,128)S(1)} %get-tuple-element.107), channel_id=1, source_target_pairs={{0,1},{1,0},{2,3},{3,2},{4,5},{5,4},{6,7},{7,6},{8,9},{9,8},{10,11... | collective-permute-start | bytes 1966088 | tf_op jit(solution)/shard_map/ppermute | solution.py:355
  86.8 10.1 %collective-permute-start.23 = (f32[1,640,128]{2,1,0:T(8,128)S(1)}, f32[1,640,128]{2,1,0:T(8,128)S(1)}, u32[]{:S(2)}, u32[]{:S(2)}) collective-permute-start(f32[1,640,128]{2,1,0:T(8,128)S(1)} %get-tuple-element.111), channel_id=1, source_target_pairs={{0,2},{1,3},{2,0},{3,1},{4,6},{5,7},{6,4},{7,5},{8,10},{9,11},{10,... | collective-permute-start | bytes 983048 | tf_op jit(solution)/shard_map/ppermute | solution.py:361
  96.9 2.5 %collective-permute-start.24 = (f32[2,1,896,128]{3,2,1,0:T(8,128)S(1)}, f32[2,1,896,128]{3,2,1,0:T(8,128)S(1)}, u32[]{:S(2)}, u32[]{:S(2)}) collective-permute-start(f32[2,1,896,128]{3,2,1,0:T(8,128)S(1)} %get-tuple-element.114), channel_id=1, source_target_pairs={{0,1},{1,0},{2,3},{3,2},{4,5},{5,4},{6,7},{7,6},{8,9},{9,8},{10,11... | collective-permute-start | bytes 2752520 | tf_op jit(solution)/shard_map/ppermute | solution.py:355
  99.4 12.6 %collective-permute-start.25 = (f32[1,896,128]{2,1,0:T(8,128)S(1)}, f32[1,896,128]{2,1,0:T(8,128)S(1)}, u32[]{:S(2)}, u32[]{:S(2)}) collective-permute-start(f32[1,896,128]{2,1,0:T(8,128)S(1)} %get-tuple-element.116), channel_id=1, source_target_pairs={{0,2},{1,3},{2,0},{3,1},{4,6},{5,7},{6,4},{7,5},{8,10},{9,11},{10,... | collective-permute-start | bytes 1376264 | tf_op jit(solution)/shard_map/ppermute | solution.py:361
  101.3 11.8 %copy-start.17 = (s32[32,1]{0,1:T(1,128)S(1)}, s32[32,1]{0,1:T(1,128)}, u32[]{:S(2)}) copy-start(s32[32,1]{0,1:T(1,128)} %param.8) | copy-start | bytes 388
  101.3 11.7 %copy-start.18 = (s32[32]{0:T(128)S(1)}, s32[32]{0:T(128)}, u32[]{:S(2)}) copy-start(s32[32]{0:T(128)} %occ.1) | copy-start | bytes 388
  101.3 11.7 %copy-start.19 = (s32[32]{0:T(128)S(1)}, s32[32]{0:T(128)}, u32[]{:S(2)}) copy-start(s32[32]{0:T(128)} %vir.1) | copy-start | bytes 388
  (3 other events, 4.9 us)

commit v4 on v3

--- a/solution.py
+++ b/solution.py
@@ -19,7 +19,7 @@
 SHIFT = 9
 MASK = (1 << SHIFT) - 1
 GROUP = 4
-SLOTS = 4
+SLOTS = 5
 AXES = ("row", "col")
 ANY = pl.BlockSpec(memory_space=pl.ANY)
 f32 = jnp.float32

time: 113 us -> 113 us (level)
  no operation moved by 1% of the time
where the time goes in v4:
time: 113 us; the launch traced here: 114 us
  waiting for transfers between devices  63.7 us (56%)
  starting transfers between devices  23.6 us (21%)
  Pallas kernels  19.3 us (17%)
  local copies, waits for them, and re-layouts  4.54 us (4%)
  other arithmetic  2.06 us (2%)
    ppermute x7, waiting for transfers between devices, overflow_round(): got.append(lax.ppermute(parts[m], AXES, pairs))  40.6 us
    ppermute x2, waiting for transfers between devices, exchange(): lax.ppermute(sums[j], 'col', [(c, (c // 2 + j) % chips * 2 + c % 2) for c...  16.1 us
    pallas_call x2, Pallas kernels, product(): pl.pallas_call(functools.partial(product_kernel, layer, firsts, low_occ,...  8.87 us
    ppermute x7, starting transfers between devices, overflow_round(): got.append(lax.ppermute(parts[m], AXES, pairs))  7.33 us
    pallas_call x1, Pallas kernels, split(): pl.pallas_call(functools.partial(split_kernel, per_step, wide, cols), gri...  5.62 us
    all_to_all x1, starting transfers between devices, body(): first = lax.all_to_all(send, AXES, split_axis=0, concat_axis=0, tiled=True)  5.59 us
    ppermute x2, waiting for transfers between devices, chip_sum(): got = lax.ppermute(give, 'col', [(c, c ^ 1) for c in range(cols)])  4.19 us
    unnamed x24, local copies, waits for them, and re-layouts  4.16 us
  transfers between devices with their start and end apart: 15, of which 10 were waited for; matrix products, arithmetic and copies ran while one was open for 1% of the time, Pallas kernels for 10%

profile of v4, /device:TPU:0, one launch (start us, length us, event | category | flops | bytes accessed | tf_op | source)
XLA Modules:
  0.0 114.1 jit_solution(8514823125612097184)
XLA Ops:
  0.0 3.7 %pack.2 = (f32[32,128,128]{2,1,0:T(8,128)}, f32[520,128]{1,0:T(8,128)S(1)}) custom-call(s32[1]{0:T(128)} %constant.67.clone.1.rnd, s32[32]{0:T(128)} %bitcast.80, s32[32]{0:T(128)} %occ.1, s32[32]{0:T(128)} %vir.1, f32[32,128,128]{2,1,0:T(8,128)} %amp.1), custom_call_target="tpu_custom_call" | custom-call | tf_op jit(solution)/shard_map/pack/pallas_call | solution.py:103
  3.7 4.1 %collective-permute-start.13 = (f32[520,128]{1,0:T(8,128)S(1)}, f32[520,128]{1,0:T(8,128)S(1)}, u32[]{:S(2)}, u32[]{:S(2)}) collective-permute-start(f32[520,128]{1,0:T(8,128)S(1)} %get-tuple-element.94.refs_0_), channel_id=1, source_target_pairs={{0,16},{1,17},{2,18},{3,19},{4,20},{5,21},{6,22},{7,23},{8,24},{9,... | collective-permute-start | bytes 798728 | tf_op jit(solution)/shard_map/ppermute | solution.py:171
  7.8 1.6 %collective-permute-start.12 = (f32[520,128]{1,0:T(8,128)S(1)}, f32[520,128]{1,0:T(8,128)S(1)}, u32[]{:S(2)}, u32[]{:S(2)}) collective-permute-start(f32[520,128]{1,0:T(8,128)S(1)} %get-tuple-element.94.refs_0_), channel_id=1, source_target_pairs={{0,8},{1,9},{2,10},{3,11},{4,12},{5,13},{6,14},{7,15},{8,0},{9,1},... | collective-permute-start | bytes 798728 | tf_op jit(solution)/shard_map/ppermute | solution.py:172
  9.5 3.4 %copy-done = f32[4096,4,128]{2,1,0:T(4,128)S(1)} copy-done((f32[4096,4,128]{2,1,0:T(4,128)S(1)}, f32[4096,4,128]{2,1,0:T(4,128)}, u32[]{:S(2)}) %copy-start) | copy-done | bytes 8388632
  12.9 5.6 %split.1.refs_9_ = bf16[32,256,512]{2,1,0:T(8,128)(2,1)} custom-call(s32[4]{0:T(128)S(1)} %pad_add_fusion.place, f32[16384,128]{1,0:T(8,128)S(1)} %bitcast.79), custom_call_target="tpu_custom_call" | custom-call | bytes 16777216 | tf_op jit(solution)/shard_map/split/pallas_call | solution.py:205
  18.5 1.5 %collective-permute-done.13.refs_2_ = f32[520,128]{1,0:T(8,128)S(1)} collective-permute-done((f32[520,128]{1,0:T(8,128)S(1)}, f32[520,128]{1,0:T(8,128)S(1)}, u32[]{:S(2)}, u32[]{:S(2)}) %collective-permute-start.13) | collective-permute-done | bytes 266272 | tf_op jit(solution)/shard_map/ppermute | solution.py:171
  20.7 5.6 %all-to-all-start = ((f32[32,128,128]{2,1,0:T(8,128)}), f32[32,128,128]{2,1,0:T(8,128)S(1)}, u32[]{:S(2)}, u32[]{:S(2)}) async-start(f32[32,128,128]{2,1,0:T(8,128)} %get-tuple-element.104), calls=%async_computation | async-start | bytes 4194304 | tf_op jit(solution)/shard_map/all_to_all | solution.py:381
  26.3 1.3 %collective-permute-done.14.refs_3_ = f32[520,128]{1,0:T(8,128)S(1)} collective-permute-done((f32[520,128]{1,0:T(8,128)S(1)}, f32[520,128]{1,0:T(8,128)S(1)}, u32[]{:S(2)}, u32[]{:S(2)}) %collective-permute-start.14) | collective-permute-done | bytes 266272 | tf_op jit(solution)/shard_map/ppermute | solution.py:174
  27.6 1.1 pick.2
  28.7 1.3 %collective-permute-start.20 = (f32[544,128]{1,0:T(8,128)S(1)}, f32[544,128]{1,0:T(8,128)S(1)}, u32[]{:S(2)}, u32[]{:S(2)}) collective-permute-start(f32[544,128]{1,0:T(8,128)S(1)} %get-tuple-element.101), channel_id=1, source_target_pairs={{0,2},{1,3},{2,0},{3,1},{4,6},{5,7},{6,4},{7,5},{8,10},{9,11},{10,... | collective-permute-start | bytes 835592 | tf_op jit(solution)/shard_map/ppermute | solution.py:180
  30.0 1.5 %collective-permute-start.18 = (f32[544,128]{1,0:T(8,128)S(1)}, f32[544,128]{1,0:T(8,128)S(1)}, u32[]{:S(2)}, u32[]{:S(2)}) collective-permute-start(f32[544,128]{1,0:T(8,128)S(1)} %get-tuple-element.99), channel_id=1, source_target_pairs={{0,4},{1,5},{2,6},{3,7},{4,0},{5,1},{6,2},{7,3},{8,12},{9,13},{10,... | collective-permute-start | bytes 835592 | tf_op jit(solution)/shard_map/ppermute | solution.py:180
  32.3 2.2 %collective-permute-start.16 = (f32[544,128]{1,0:T(8,128)S(1)}, f32[544,128]{1,0:T(8,128)S(1)}, u32[]{:S(2)}, u32[]{:S(2)}) collective-permute-start(f32[544,128]{1,0:T(8,128)S(1)} %get-tuple-element.97), channel_id=1, source_target_pairs={{0,6},{1,7},{2,4},{3,5},{4,2},{5,3},{6,0},{7,1},{8,14},{9,15},{10,... | collective-permute-start | bytes 835592 | tf_op jit(solution)/shard_map/ppermute | solution.py:180
  34.5 19.2 %collective-permute-done.20.refs_5_ = f32[544,128]{1,0:T(8,128)S(1)} collective-permute-done((f32[544,128]{1,0:T(8,128)S(1)}, f32[544,128]{1,0:T(8,128)S(1)}, u32[]{:S(2)}, u32[]{:S(2)}) %collective-permute-start.20) | collective-permute-done | bytes 278560 | tf_op jit(solution)/shard_map/ppermute | solution.py:180
  54.0 6.2 %collective-permute-done.19.refs_4_ = f32[544,128]{1,0:T(8,128)S(1)} collective-permute-done((f32[544,128]{1,0:T(8,128)S(1)}, f32[544,128]{1,0:T(8,128)S(1)}, u32[]{:S(2)}, u32[]{:S(2)}) %collective-permute-start.19) | collective-permute-done | bytes 278560 | tf_op jit(solution)/shard_map/ppermute | solution.py:180
  60.2 1.1 collective-permute-start.21
  61.4 9.4 %collective-permute-done.16.refs_1_ = f32[544,128]{1,0:T(8,128)S(1)} collective-permute-done((f32[544,128]{1,0:T(8,128)S(1)}, f32[544,128]{1,0:T(8,128)S(1)}, u32[]{:S(2)}, u32[]{:S(2)}) %collective-permute-start.16) | collective-permute-done | bytes 278560 | tf_op jit(solution)/shard_map/ppermute | solution.py:180
  70.8 5.8 %collective-permute-done.15.refs_0_ = f32[544,128]{1,0:T(8,128)S(1)} collective-permute-done((f32[544,128]{1,0:T(8,128)S(1)}, f32[544,128]{1,0:T(8,128)S(1)}, u32[]{:S(2)}, u32[]{:S(2)}) %collective-permute-start.15) | collective-permute-done | bytes 278560 | tf_op jit(solution)/shard_map/ppermute | solution.py:180
  77.8 4.4 %product.3 = (f32[2,1,640,128]{3,2,1,0:T(8,128)S(1)}, f32[2,1,640,128]{3,2,1,0:T(8,128)S(1)}) custom-call(s32[1]{0:T(128)} %constant.67.clone.1.rnd, s32[4]{0:T(128)S(1)} %pad_add_fusion.place, s32[32]{0:T(128)S(1)} %reshape.169.table, f32[544,128]{1,0:T(8,128)} %copy-done.15, f32[544,128]{1,0:T(8,128)} %copy-done.14, f32[544,128]{1,0:T(8,128)} %copy-done.13, ...), custom_call_target="tpu_custom_call" | custom-call | flops 1073741824 | bytes 16777216 | tf_op jit(solution)/shard_map/product/pallas_call | solution.py:333
  82.3 3.8 %collective-permute-start.22 = (f32[2,1,640,128]{3,2,1,0:T(8,128)S(1)}, f32[2,1,640,128]{3,2,1,0:T(8,128)S(1)}, u32[]{:S(2)}, u32[]{:S(2)}) collective-permute-start(f32[2,1,640,128]{3,2,1,0:T(8,128)S(1)} %get-tuple-element.107), channel_id=1, source_target_pairs={{0,1},{1,0},{2,3},{3,2},{4,5},{5,4},{6,7},{7,6},{8,9},{9,8},{10,11... | collective-permute-start | bytes 1966088 | tf_op jit(solution)/shard_map/ppermute | solution.py:355
  86.1 1.7 %collective-permute-done.22 = f32[2,1,640,128]{3,2,1,0:T(8,128)S(1)} collective-permute-done((f32[2,1,640,128]{3,2,1,0:T(8,128)S(1)}, f32[2,1,640,128]{3,2,1,0:T(8,128)S(1)}, u32[]{:S(2)}, u32[]{:S(2)}) %collective-permute-start.22) | collective-permute-done | bytes 655392 | tf_op jit(solution)/shard_map/ppermute | solution.py:355
  87.9 4.4 %product.4 = (f32[2,1,896,128]{3,2,1,0:T(8,128)S(1)}, f32[2,1,896,128]{3,2,1,0:T(8,128)S(1)}) custom-call(s32[1]{0:T(128)} %constant.67.clone.1.rnd, s32[4]{0:T(128)S(1)} %pad_add_fusion.place, s32[32]{0:T(128)S(1)} %reshape.169.table, f32[544,128]{1,0:T(8,128)} %copy-done.15, f32[544,128]{1,0:T(8,128)} %copy-done.14, f32[544,128]{1,0:T(8,128)} %copy-done.13, ...), custom_call_target="tpu_custom_call" | custom-call | flops 1073741824 | bytes 16777216 | tf_op jit(solution)/shard_map/product/pallas_call | solution.py:333
  92.4 5.5 %collective-permute-done.23 = f32[1,640,128]{2,1,0:T(8,128)S(1)} collective-permute-done((f32[1,640,128]{2,1,0:T(8,128)S(1)}, f32[1,640,128]{2,1,0:T(8,128)S(1)}, u32[]{:S(2)}, u32[]{:S(2)}) %collective-permute-start.23) | collective-permute-done | bytes 327712 | tf_op jit(solution)/shard_map/ppermute | solution.py:361
  97.9 2.5 %collective-permute-done.24 = f32[2,1,896,128]{3,2,1,0:T(8,128)S(1)} collective-permute-done((f32[2,1,896,128]{3,2,1,0:T(8,128)S(1)}, f32[2,1,896,128]{3,2,1,0:T(8,128)S(1)}, u32[]{:S(2)}, u32[]{:S(2)}) %collective-permute-start.24) | collective-permute-done | bytes 917536 | tf_op jit(solution)/shard_map/ppermute | solution.py:355
  102.5 10.6 %collective-permute-done.25 = f32[1,896,128]{2,1,0:T(8,128)S(1)} collective-permute-done((f32[1,896,128]{2,1,0:T(8,128)S(1)}, f32[1,896,128]{2,1,0:T(8,128)S(1)}, u32[]{:S(2)}, u32[]{:S(2)}) %collective-permute-start.25) | collective-permute-done | bytes 458784 | tf_op jit(solution)/shard_map/ppermute | solution.py:361
  (70 shorter events, 5.6 us)
Async XLA Ops:
  3.7 16.3 %collective-permute-start.13 = (f32[520,128]{1,0:T(8,128)S(1)}, f32[520,128]{1,0:T(8,128)S(1)}, u32[]{:S(2)}, u32[]{:S(2)}) collective-permute-start(f32[520,128]{1,0:T(8,128)S(1)} %get-tuple-element.94.refs_0_), channel_id=1, source_target_pairs={{0,16},{1,17},{2,18},{3,19},{4,20},{5,21},{6,22},{7,23},{8,24},{9,... | collective-permute-start | bytes 798728 | tf_op jit(solution)/shard_map/ppermute | solution.py:171
  7.8 18.5 %collective-permute-start.12 = (f32[520,128]{1,0:T(8,128)S(1)}, f32[520,128]{1,0:T(8,128)S(1)}, u32[]{:S(2)}, u32[]{:S(2)}) collective-permute-start(f32[520,128]{1,0:T(8,128)S(1)} %get-tuple-element.94.refs_0_), channel_id=1, source_target_pairs={{0,8},{1,9},{2,10},{3,11},{4,12},{5,13},{6,14},{7,15},{8,0},{9,1},... | collective-permute-start | bytes 798728 | tf_op jit(solution)/shard_map/ppermute | solution.py:172
  20.0 7.6 %collective-permute-start.14 = (f32[520,128]{1,0:T(8,128)S(1)}, f32[520,128]{1,0:T(8,128)S(1)}, u32[]{:S(2)}, u32[]{:S(2)}) collective-permute-start(f32[520,128]{1,0:T(8,128)S(1)} %collective-permute-done.13.refs_2_), channel_id=1, source_target_pairs={{0,8},{1,9},{2,10},{3,11},{4,12},{5,13},{6,14},{7,15},{8,0},{9,1},... | collective-permute-start | bytes 798728 | tf_op jit(solution)/shard_map/ppermute | solution.py:174
  20.7 57.1 %all-to-all-start = ((f32[32,128,128]{2,1,0:T(8,128)}), f32[32,128,128]{2,1,0:T(8,128)S(1)}, u32[]{:S(2)}, u32[]{:S(2)}) async-start(f32[32,128,128]{2,1,0:T(8,128)} %get-tuple-element.104), calls=%async_computation | async-start | bytes 4194304 | tf_op jit(solution)/shard_map/all_to_all | solution.py:381
  28.7 49.2 %copy-start.2 = (f32[544,128]{1,0:T(8,128)}, f32[544,128]{1,0:T(8,128)S(1)}, u32[]{:S(2)}) copy-start(f32[544,128]{1,0:T(8,128)S(1)} %get-tuple-element.103.refs_7_) | copy-start | bytes 835588
  28.7 25.0 %collective-permute-start.20 = (f32[544,128]{1,0:T(8,128)S(1)}, f32[544,128]{1,0:T(8,128)S(1)}, u32[]{:S(2)}, u32[]{:S(2)}) collective-permute-start(f32[544,128]{1,0:T(8,128)S(1)} %get-tuple-element.101), channel_id=1, source_target_pairs={{0,2},{1,3},{2,0},{3,1},{4,6},{5,7},{6,4},{7,5},{8,10},{9,11},{10,... | collective-permute-start | bytes 835592 | tf_op jit(solution)/shard_map/ppermute | solution.py:180
  30.0 30.2 %collective-permute-start.19 = (f32[544,128]{1,0:T(8,128)S(1)}, f32[544,128]{1,0:T(8,128)S(1)}, u32[]{:S(2)}, u32[]{:S(2)}) collective-permute-start(f32[544,128]{1,0:T(8,128)S(1)} %get-tuple-element.100), channel_id=1, source_target_pairs={{0,3},{1,2},{2,1},{3,0},{4,7},{5,6},{6,5},{7,4},{8,11},{9,10},{10,... | collective-permute-start | bytes 835592 | tf_op jit(solution)/shard_map/ppermute | solution.py:180
  30.0 31.4 %collective-permute-start.18 = (f32[544,128]{1,0:T(8,128)S(1)}, f32[544,128]{1,0:T(8,128)S(1)}, u32[]{:S(2)}, u32[]{:S(2)}) collective-permute-start(f32[544,128]{1,0:T(8,128)S(1)} %get-tuple-element.99), channel_id=1, source_target_pairs={{0,4},{1,5},{2,6},{3,7},{4,0},{5,1},{6,2},{7,3},{8,12},{9,13},{10,... | collective-permute-start | bytes 835592 | tf_op jit(solution)/shard_map/ppermute | solution.py:180
  31.5 29.9 %collective-permute-start.17 = (f32[544,128]{1,0:T(8,128)S(1)}, f32[544,128]{1,0:T(8,128)S(1)}, u32[]{:S(2)}, u32[]{:S(2)}) collective-permute-start(f32[544,128]{1,0:T(8,128)S(1)} %get-tuple-element.98), channel_id=1, source_target_pairs={{0,5},{1,4},{2,7},{3,6},{4,1},{5,0},{6,3},{7,2},{8,13},{9,12},{10,... | collective-permute-start | bytes 835592 | tf_op jit(solution)/shard_map/ppermute | solution.py:180
  32.3 38.6 %collective-permute-start.16 = (f32[544,128]{1,0:T(8,128)S(1)}, f32[544,128]{1,0:T(8,128)S(1)}, u32[]{:S(2)}, u32[]{:S(2)}) collective-permute-start(f32[544,128]{1,0:T(8,128)S(1)} %get-tuple-element.97), channel_id=1, source_target_pairs={{0,6},{1,7},{2,4},{3,5},{4,2},{5,3},{6,0},{7,1},{8,14},{9,15},{10,... | collective-permute-start | bytes 835592 | tf_op jit(solution)/shard_map/ppermute | solution.py:180
  53.7 24.2 %copy-start.10 = (f32[544,128]{1,0:T(8,128)}, f32[544,128]{1,0:T(8,128)S(1)}, u32[]{:S(2)}) copy-start(f32[544,128]{1,0:T(8,128)S(1)} %collective-permute-done.20.refs_5_) | copy-start | bytes 835588
  53.7 23.0 %collective-permute-start.15 = (f32[544,128]{1,0:T(8,128)S(1)}, f32[544,128]{1,0:T(8,128)S(1)}, u32[]{:S(2)}, u32[]{:S(2)}) collective-permute-start(f32[544,128]{1,0:T(8,128)S(1)} %get-tuple-element.96), channel_id=1, source_target_pairs={{0,7},{1,6},{2,5},{3,4},{4,3},{5,2},{6,1},{7,0},{8,15},{9,14},{10,... | collective-permute-start | bytes 835592 | tf_op jit(solution)/shard_map/ppermute | solution.py:180
  60.2 17.6 %copy-start.11 = (f32[544,128]{1,0:T(8,128)}, f32[544,128]{1,0:T(8,128)S(1)}, u32[]{:S(2)}) copy-start(f32[544,128]{1,0:T(8,128)S(1)} %collective-permute-done.19.refs_4_) | copy-start | bytes 835588
  60.2 16.4 %collective-permute-start.21 = (f32[544,128]{1,0:T(8,128)S(1)}, f32[544,128]{1,0:T(8,128)S(1)}, u32[]{:S(2)}, u32[]{:S(2)}) collective-permute-start(f32[544,128]{1,0:T(8,128)S(1)} %get-tuple-element.102), channel_id=1, source_target_pairs={{0,1},{1,0},{2,3},{3,2},{4,5},{5,4},{6,7},{7,6},{8,9},{9,8},{10,11... | collective-permute-start | bytes 835592 | tf_op jit(solution)/shard_map/ppermute | solution.py:180
  61.4 16.4 %copy-start.12 = (f32[544,128]{1,0:T(8,128)}, f32[544,128]{1,0:T(8,128)S(1)}, u32[]{:S(2)}) copy-start(f32[544,128]{1,0:T(8,128)S(1)} %collective-permute-done.18.refs_3_) | copy-start | bytes 835588
  61.4 15.3 %copy-start.13 = (f32[544,128]{1,0:T(8,128)}, f32[544,128]{1,0:T(8,128)S(1)}, u32[]{:S(2)}) copy-start(f32[544,128]{1,0:T(8,128)S(1)} %collective-permute-done.17.refs_2_) | copy-start | bytes 835588
  70.8 5.9 %copy-start.14 = (f32[544,128]{1,0:T(8,128)}, f32[544,128]{1,0:T(8,128)S(1)}, u32[]{:S(2)}) copy-start(f32[544,128]{1,0:T(8,128)S(1)} %collective-permute-done.16.refs_1_) | copy-start | bytes 835588
  82.3 5.5 %collective-permute-start.22 = (f32[2,1,640,128]{3,2,1,0:T(8,128)S(1)}, f32[2,1,640,128]{3,2,1,0:T(8,128)S(1)}, u32[]{:S(2)}, u32[]{:S(2)}) collective-permute-start(f32[2,1,640,128]{3,2,1,0:T(8,128)S(1)} %get-tuple-element.107), channel_id=1, source_target_pairs={{0,1},{1,0},{2,3},{3,2},{4,5},{5,4},{6,7},{7,6},{8,9},{9,8},{10,11... | collective-permute-start | bytes 1966088 | tf_op jit(solution)/shard_map/ppermute | solution.py:355
  87.9 10.1 %collective-permute-start.23 = (f32[1,640,128]{2,1,0:T(8,128)S(1)}, f32[1,640,128]{2,1,0:T(8,128)S(1)}, u32[]{:S(2)}, u32[]{:S(2)}) collective-permute-start(f32[1,640,128]{2,1,0:T(8,128)S(1)} %get-tuple-element.111), channel_id=1, source_target_pairs={{0,2},{1,3},{2,0},{3,1},{4,6},{5,7},{6,4},{7,5},{8,10},{9,11},{10,... | collective-permute-start | bytes 983048 | tf_op jit(solution)/shard_map/ppermute | solution.py:361
  97.9 2.5 %collective-permute-start.24 = (f32[2,1,896,128]{3,2,1,0:T(8,128)S(1)}, f32[2,1,896,128]{3,2,1,0:T(8,128)S(1)}, u32[]{:S(2)}, u32[]{:S(2)}) collective-permute-start(f32[2,1,896,128]{3,2,1,0:T(8,128)S(1)} %get-tuple-element.114), channel_id=1, source_target_pairs={{0,1},{1,0},{2,3},{3,2},{4,5},{5,4},{6,7},{7,6},{8,9},{9,8},{10,11... | collective-permute-start | bytes 2752520 | tf_op jit(solution)/shard_map/ppermute | solution.py:355
  100.5 12.6 %collective-permute-start.25 = (f32[1,896,128]{2,1,0:T(8,128)S(1)}, f32[1,896,128]{2,1,0:T(8,128)S(1)}, u32[]{:S(2)}, u32[]{:S(2)}) collective-permute-start(f32[1,896,128]{2,1,0:T(8,128)S(1)} %get-tuple-element.116), channel_id=1, source_target_pairs={{0,2},{1,3},{2,0},{3,1},{4,6},{5,7},{6,4},{7,5},{8,10},{9,11},{10,... | collective-permute-start | bytes 1376264 | tf_op jit(solution)/shard_map/ppermute | solution.py:361
  102.5 11.6 %copy-start.17 = (s32[32,1]{0,1:T(1,128)S(1)}, s32[32,1]{0,1:T(1,128)}, u32[]{:S(2)}) copy-start(s32[32,1]{0,1:T(1,128)} %param.8) | copy-start | bytes 388
  102.5 11.6 %copy-start.18 = (s32[32]{0:T(128)S(1)}, s32[32]{0:T(128)}, u32[]{:S(2)}) copy-start(s32[32]{0:T(128)} %occ.1) | copy-start | bytes 388
  102.5 11.6 %copy-start.19 = (s32[32]{0:T(128)S(1)}, s32[32]{0:T(128)}, u32[]{:S(2)}) copy-start(s32[32]{0:T(128)} %vir.1) | copy-start | bytes 388
  (3 other events, 4.9 us)
